TPU v7x, 256 devices: a whole 4x4x8 slice. The times are simulated.
256 devices in a mesh: rows: 128 (over y, x, z_hi, core), batch: 2 (over z_lo).
Axes of the slice: x: 4, y: 4, z: 8 (z_hi: 4, z_lo: 2; z = z_hi * 2 + z_lo), core: 2. Of those that a mesh axis runs over, the one named last changes fastest.
Arguments:
- features: bfloat16 [2, 512, 512, 128], P('batch', 'rows'), may hold values from -64 to 64
- grad_out: bfloat16 [2, 512, 512, 128], P('batch', 'rows'), may hold values from -6 to 6
- qkv_weight: bfloat16 [128, 384], replicated, may hold values from -8 to 8
- proj_weight: bfloat16 [128, 128], replicated, may hold values from -0.5 to 0.5
- lepe_weight: bfloat16 [9, 128], replicated, may hold values from -2 to 2
Outputs:
- grad_features: bfloat16 [2, 512, 512, 128], P('batch', 'rows')
- grad_qkv: float32 [128, 384], replicated
- grad_proj: float32 [128, 128], replicated
- grad_lepe: float32 [9, 128], replicated
All inputs are finite; a program needn't handle non-finite values.
Results may differ from a plain program's by a relative error of at most 0.0055.
The roundings to bfloat16 on the way count: a program that leaves them out, or rounds other values in their place, can miss the bound.
Values may be sent and summed in bfloat16 or wider, within the bound.
A program may use at most 64 MiB of HBM per device.

v0:
```python
import math

import jax
import jax.numpy as jnp
from jax import lax
from jax.sharding import PartitionSpec as P

NUM_HEADS = 4
STRIPE = 2


EPSILON = 1e-05


def stripe_head(queries, key_rows, values, grad_rows):
    length = queries.shape[0]
    head_size = queries.shape[1]
    block_rows = math.gcd(length, 512)
    block_count = length // block_rows
    score_scale = head_size ** (-0.5)
    query_blocks = queries.reshape(block_count, block_rows, head_size)
    grad_blocks = grad_rows.reshape(block_count, block_rows, head_size)

    def advance(carry, pieces):
        key_grad, value_grad = carry
        query_block, grad_block = pieces
        scores = jnp.dot(query_block, key_rows.T, preferred_element_type=jnp.float32) * score_scale
        row_max = jnp.max(scores, axis=1, keepdims=True)
        raised = jnp.exp(scores - row_max)
        probs_full = raised / jnp.sum(raised, axis=1, keepdims=True)
        probs_low = probs_full.astype(jnp.bfloat16)
        out_block = jnp.dot(probs_low, values, preferred_element_type=jnp.float32)
        grad_probs = jnp.dot(grad_block, values.T, preferred_element_type=jnp.float32)
        row_inner = jnp.sum(probs_full * grad_probs, axis=1, keepdims=True)
        grad_scores = (probs_full * (grad_probs - row_inner) * score_scale).astype(jnp.bfloat16)
        query_grad = jnp.dot(grad_scores, key_rows, preferred_element_type=jnp.float32)
        key_grad = key_grad + jnp.dot(
            grad_scores.T, query_block, preferred_element_type=jnp.float32
        )
        value_grad = value_grad + jnp.dot(
            probs_low.T, grad_block, preferred_element_type=jnp.float32
        )
        return ((key_grad, value_grad), (out_block, query_grad))

    zeros_init = jnp.zeros((length, head_size), jnp.float32)
    (key_grad, value_grad), (out_blocks, query_grads) = lax.scan(
        advance, (zeros_init, zeros_init), (query_blocks, grad_blocks)
    )
    return (
        out_blocks.reshape(length, head_size),
        query_grads.reshape(length, head_size),
        key_grad,
        value_grad,
    )


def stripes_backward(qkv_rows, grad_rows, head_size):
    group_count, length, triple = qkv_rows.shape
    half_width = triple // 3
    heads_here = half_width // head_size

    def split_heads(packed):
        return (
            packed.reshape(group_count, length, heads_here, head_size)
            .transpose(0, 2, 1, 3)
            .reshape(group_count * heads_here, length, head_size)
        )

    def merge_heads(items):
        return (
            items.reshape(group_count, heads_here, length, head_size)
            .transpose(0, 2, 1, 3)
            .reshape(group_count, length, half_width)
        )

    pieces = (
        split_heads(qkv_rows[:, :, :half_width]),
        split_heads(qkv_rows[:, :, half_width : 2 * half_width]),
        split_heads(qkv_rows[:, :, 2 * half_width :]),
        split_heads(grad_rows),
    )
    results = lax.map(lambda item_parts: stripe_head(*item_parts), pieces)
    return tuple((merge_heads(result) for result in results))


def lepe_terms(values_pad, grad_pad, weights, row_axis, col_axis):
    row_count = values_pad.shape[row_axis] - 2
    col_count = values_pad.shape[col_axis] - 2

    def window(source, row_off, col_off):
        sliced = lax.slice_in_dim(source, 1 + row_off, 1 + row_off + row_count, axis=row_axis)
        return lax.slice_in_dim(sliced, 1 + col_off, 1 + col_off + col_count, axis=col_axis)

    values_wide = values_pad.astype(jnp.float32)
    grad_wide = grad_pad.astype(jnp.float32)
    centre = window(grad_wide, 0, 0)
    summed_axes = tuple(range(values_pad.ndim - 1))
    lepe_out = jnp.zeros(centre.shape, jnp.float32)
    grad_values = jnp.zeros(centre.shape, jnp.float32)
    grad_list = []
    for row_off in (-1, 0, 1):
        for col_off in (-1, 0, 1):
            tap_weight = weights[(row_off + 1) * 3 + col_off + 1]
            shifted = window(values_wide, row_off, col_off)
            lepe_out = lepe_out + tap_weight * shifted
            grad_values = grad_values + tap_weight * window(grad_wide, -row_off, -col_off)
            grad_list.append(jnp.sum(centre * shifted, axis=summed_axes))
    return (lepe_out, grad_values, jnp.stack(grad_list))


def body(features, grad_out, qkv_weight, proj_weight, lepe_weight):
    band_rows = features.shape[1]
    map_cols = features.shape[2]
    channels = features.shape[3]
    half_width = channels // 2
    head_size = channels // NUM_HEADS
    devices_rows = lax.axis_size("rows")
    group_dev = map_cols // devices_rows // STRIPE
    contract_rows = (((0,), (0,)), ((), ()))
    contract_cols = (((1,), (1,)), ((), ()))
    tokens_flat = features.reshape(-1, channels).astype(jnp.float32)
    centred = tokens_flat - jnp.mean(tokens_flat, axis=1, keepdims=True)
    inv_std = lax.rsqrt(jnp.mean(centred * centred, axis=1, keepdims=True) + EPSILON)
    unit_norm = centred * inv_std
    normed = unit_norm.astype(jnp.bfloat16)
    w_horiz = jnp.concatenate(
        [
            qkv_weight[:, 0:half_width],
            qkv_weight[:, channels : channels + half_width],
            qkv_weight[:, 2 * channels : 2 * channels + half_width],
        ],
        axis=1,
    )
    w_vert = jnp.concatenate(
        [
            qkv_weight[:, half_width:channels],
            qkv_weight[:, channels + half_width : 2 * channels],
            qkv_weight[:, 2 * channels + half_width :],
        ],
        axis=1,
    )
    qkv_horiz = jnp.dot(normed, w_horiz, preferred_element_type=jnp.float32).astype(jnp.bfloat16)
    grad_flat = grad_out.reshape(-1, channels)
    grad_attn = lax.dot_general(
        grad_flat, proj_weight, contract_cols, preferred_element_type=jnp.float32
    ).astype(jnp.bfloat16)
    weights_wide = lepe_weight.astype(jnp.float32)
    weights_vert = weights_wide[:, half_width:]
    pad_window = ((0, 0), (1, 1), (1, 1), (0, 0))
    grad_vert = grad_attn[:, half_width:].reshape(
        band_rows, devices_rows, group_dev, STRIPE * half_width
    )
    first_part = (
        jnp.dot(normed, w_vert, preferred_element_type=jnp.float32)
        .astype(jnp.bfloat16)
        .reshape(band_rows, devices_rows, group_dev, STRIPE * 3 * half_width)
    )
    first_cols = lax.all_to_all(first_part, "rows", split_axis=1, concat_axis=0, tiled=True)
    grad_cols = lax.all_to_all(grad_vert, "rows", split_axis=1, concat_axis=0, tiled=True)
    map_rows = first_cols.shape[0]
    items = first_cols.shape[2]
    qkv_cols = first_cols
    qkv_cols = qkv_cols.reshape(map_rows, items, STRIPE, 3 * half_width).transpose(1, 0, 2, 3)
    grad_stripes = grad_cols.reshape(map_rows, items, STRIPE, half_width).transpose(1, 0, 2, 3)
    col_length = map_rows * STRIPE
    attn_v, query_v, key_v, value_v = stripes_backward(
        qkv_cols.reshape(items, col_length, 3 * half_width),
        grad_stripes.reshape(items, col_length, half_width),
        head_size,
    )
    lepe_v, lepe_grad_v, tap_grad_v = jax.vmap(
        lambda value_item, grad_item: lepe_terms(value_item, grad_item, weights_vert, 0, 1)
    )(jnp.pad(qkv_cols[..., 2 * half_width :], pad_window), jnp.pad(grad_stripes, pad_window))
    col_shape = (items, map_rows, STRIPE, half_width)
    back_rows = jnp.concatenate(
        [
            query_v.reshape(col_shape),
            key_v.reshape(col_shape),
            value_v.reshape(col_shape) + lepe_grad_v,
            attn_v.reshape(col_shape) + lepe_v,
        ],
        axis=3,
    ).astype(jnp.bfloat16)
    back_rows = back_rows.transpose(1, 0, 2, 3).reshape(map_rows, 1, items, STRIPE * 4 * half_width)
    returned = lax.all_to_all(back_rows, "rows", split_axis=0, concat_axis=1, tiled=True)
    returned, tap_parts = (returned, tap_grad_v.reshape(1, 1, items, 9, half_width))
    group_count = band_rows // STRIPE
    length = STRIPE * map_cols
    attn_h, query_h, key_h, value_h = stripes_backward(
        qkv_horiz.reshape(group_count, length, 3 * half_width),
        grad_attn[:, :half_width].reshape(group_count, length, half_width),
        head_size,
    )
    window_shape = (group_count, STRIPE, map_cols, half_width)
    lepe_h, lepe_grad_h, tap_grad_h = lepe_terms(
        jnp.pad(qkv_horiz[:, 2 * half_width :].reshape(window_shape), pad_window),
        jnp.pad(grad_attn[:, :half_width].reshape(window_shape), pad_window),
        weights_wide[:, :half_width],
        1,
        2,
    )

    def flat_rows(source):
        return source.reshape(band_rows * map_cols, half_width)

    back_flat = returned.reshape(band_rows * map_cols, 4 * half_width)
    attn = jnp.concatenate(
        [
            (flat_rows(attn_h) + flat_rows(lepe_h)).astype(jnp.bfloat16),
            back_flat[:, 3 * half_width :],
        ],
        axis=1,
    )
    grad_tokens = jnp.concatenate(
        [
            flat_rows(query_h).astype(jnp.bfloat16),
            back_flat[:, :half_width],
            flat_rows(key_h).astype(jnp.bfloat16),
            back_flat[:, half_width : 2 * half_width],
            (flat_rows(value_h) + flat_rows(lepe_grad_h)).astype(jnp.bfloat16),
            back_flat[:, 2 * half_width : 3 * half_width],
        ],
        axis=1,
    )
    grad_proj_part = lax.dot_general(
        attn, grad_flat, contract_rows, preferred_element_type=jnp.float32
    )
    grad_qkv_part = lax.dot_general(
        normed, grad_tokens, contract_rows, preferred_element_type=jnp.float32
    )
    grad_unit = lax.dot_general(
        grad_tokens, qkv_weight, contract_cols, preferred_element_type=jnp.float32
    )
    grad_norm = (
        grad_unit
        - jnp.mean(grad_unit, axis=1, keepdims=True)
        - unit_norm * jnp.mean(grad_unit * unit_norm, axis=1, keepdims=True)
    ) * inv_std
    grad_features = (
        (grad_flat.astype(jnp.float32) + grad_norm)
        .astype(jnp.bfloat16)
        .reshape(1, band_rows, map_cols, channels)
    )
    tap_total = jnp.concatenate([tap_grad_h, jnp.sum(tap_parts, axis=(0, 1, 2))], axis=1)
    summed = lax.psum((grad_qkv_part, grad_proj_part, tap_total), ("rows", "batch"))
    total_tokens = lax.axis_size("batch") * devices_rows * band_rows * map_cols
    grad_scale = total_tokens ** (-0.5)
    return (grad_features, summed[0] * grad_scale, summed[1] * grad_scale, summed[2] * grad_scale)


def solution(mesh):
    in_specs = (P("batch", "rows", None, None), P("batch", "rows", None, None), P(), P(), P())
    out_specs = (P("batch", "rows", None, None), P(), P(), P())
    return jax.shard_map(body, mesh=mesh, in_specs=in_specs, out_specs=out_specs, check_vma=False)
```

profile of v0, /device:TPU:1, one launch (start us, length us, event | category | flops | bytes accessed | tf_op | source)
XLA Modules:
  0.0 643.7 jit_solution(16351815542564240466)
XLA Ops:
  10.8 17.2 %all-to-all-start.1 = ((bf16[4,128,2,128]{3,2,0,1:T(2,128)(2,1)}), bf16[4,128,2,128]{3,2,0,1:T(2,128)(2,1)}, u32[]{:S(2)}, u32[]{:S(2)}) async-start(bf16[4,128,2,128]{3,2,0,1:T(2,128)(2,1)} %copy.266), calls=%async_computation.1 | async-start | bytes 524288 | tf_op jit(solution)/shard_map/all_to_all | solution.py:159
  44.6 61.2 %while.67 = (s32[]{:T(128)}, f32[4,1024,32]{2,1,0:T(8,128)}, bf16[4,1024,32]{2,1,0:T(8,128)(2,1)S(1)}, bf16[4,1024,32]{1,2,0:T(8,128)(2,1)}, f32[4,1024,32]{1,2,...) while((s32[]{:T(128)}, f32[4,1024,32]{2,1,0:T(8,128)}, ...), condition=%wide.region_8.9_spmd, body=%wide.region_2.8_spmd.sunk | while | flops 209844736 | bytes 27933132 | solution.py:82
  46.7 9.7 %while.70 = (s32[]{:T(128)}, f32[1024,32]{0,1:T(8,128)S(1)}, f32[1024,32]{0,1:T(8,128)S(1)}, f32[2,512,32]{1,2,0:T(8,128)}, bf16[2,512,32]{1,2,0:T(8,128)(2,1)S(...) while((s32[]{:T(128)}, f32[1024,32]{0,1:T(8,128)S(1)}, ...), condition=%wide.region_7.7_spmd.clone, body=%wide.region_3.6_spmd.clone.sunk | while | flops 209844736 | bytes 25311440 | solution.py:46
  61.9 9.8 %while.70 = (s32[]{:T(128)}, f32[1024,32]{0,1:T(8,128)S(1)}, f32[1024,32]{0,1:T(8,128)S(1)}, f32[2,512,32]{1,2,0:T(8,128)}, bf16[2,512,32]{1,2,0:T(8,128)(2,1)S(...) while((s32[]{:T(128)}, f32[1024,32]{0,1:T(8,128)S(1)}, ...), condition=%wide.region_7.7_spmd.clone, body=%wide.region_3.6_spmd.clone.sunk | while | flops 209844736 | bytes 25311440 | solution.py:46
  77.2 9.8 %while.70 = (s32[]{:T(128)}, f32[1024,32]{0,1:T(8,128)S(1)}, f32[1024,32]{0,1:T(8,128)S(1)}, f32[2,512,32]{1,2,0:T(8,128)}, bf16[2,512,32]{1,2,0:T(8,128)(2,1)S(...) while((s32[]{:T(128)}, f32[1024,32]{0,1:T(8,128)S(1)}, ...), condition=%wide.region_7.7_spmd.clone, body=%wide.region_3.6_spmd.clone.sunk | while | flops 209844736 | bytes 25311440 | solution.py:46
  92.5 9.8 %while.70 = (s32[]{:T(128)}, f32[1024,32]{0,1:T(8,128)S(1)}, f32[1024,32]{0,1:T(8,128)S(1)}, f32[2,512,32]{1,2,0:T(8,128)}, bf16[2,512,32]{1,2,0:T(8,128)(2,1)S(...) while((s32[]{:T(128)}, f32[1024,32]{0,1:T(8,128)S(1)}, ...), condition=%wide.region_7.7_spmd.clone, body=%wide.region_3.6_spmd.clone.sunk | while | flops 209844736 | bytes 25311440 | solution.py:46
  113.5 14.9 %all-to-all-start = ((bf16[4,128,2,384]{3,2,0,1:T(2,128)(2,1)}), bf16[4,128,2,384]{3,2,0,1:T(2,128)(2,1)}, u32[]{:S(2)}, u32[]{:S(2)}) async-start(bf16[4,128,2,384]{3,2,0,1:T(2,128)(2,1)} %copy.261), calls=%async_computation | async-start | bytes 1572864 | tf_op jit(solution)/shard_map/all_to_all | solution.py:158
  131.3 2.6 copy.295
  148.8 2.5 fusion.40
  154.9 3.6 reshape.211
  161.2 3.0 fusion.85
  164.2 9.6 %pad_maximum_fusion.2 = bf16[2,2048,32]{2,0,1:T(2,128)(2,1)S(1)} fusion(bf16[2,1024,32]{2,0,1:T(2,128)(2,1)S(1)} %get-tuple-element.517, bf16[2,1024,32]{2,0,1:T(2,128)(2,1)S(1)} %get-tuple-element.516), kind=kLoop, calls=%fused_computation.78 | loop fusion | flops 131072 | bytes 524288 | tf_op jit(solution)/shard_map/concatenate.5
  174.9 9.7 %pad_maximum_fusion = (bf16[2,2048,32]{2,0,1:T(2,128)(2,1)S(1)}, bf16[2,2048,32]{2,0,1:T(2,128)(2,1)S(1)}) fusion(bf16[2,1024,32]{2,0,1:T(2,128)(2,1)S(1)} %get-tuple-element.520, bf16[2,1024,32]{2,0,1:T(2,128)(2,1)S(1)} %get-tuple-element.521, bf16[2,1024,32]{2,0,1:T(2,128)(2,1)S(1)} %get-tuple-element.518, bf16[2,1024,32]{2,0,1:T(2,128)(2,1)S(1)} %get-tuple-element.519), kind=kLoop, calls=%fused_computation.76 | loop fusion | flops 262144 | bytes 1048576 | tf_op jit(solution)/shard_map/concatenate.3
  189.2 61.4 %while.69 = (s32[]{:T(128)}, f32[4,1024,32]{2,1,0:T(8,128)}, bf16[4,1024,32]{2,1,0:T(8,128)(2,1)S(1)}, bf16[4,1024,32]{1,2,0:T(8,128)(2,1)}, f32[4,1024,32]{1,2,...) while((s32[]{:T(128)}, f32[4,1024,32]{2,1,0:T(8,128)}, ...), condition=%wide.region_15.16_spmd, body=%wide.region_9.0_spmd.sunk | while | flops 209844736 | bytes 27933132 | solution.py:82
  191.6 9.7 %while.71 = (s32[]{:T(128)}, f32[1024,32]{0,1:T(8,128)S(1)}, f32[1024,32]{0,1:T(8,128)S(1)}, f32[2,512,32]{1,2,0:T(8,128)}, bf16[2,512,32]{1,2,0:T(8,128)(2,1)S(...) while((s32[]{:T(128)}, f32[1024,32]{0,1:T(8,128)S(1)}, ...), condition=%wide.region_14.14_spmd.clone, body=%wide.region_10.13_spmd.clone.sunk | while | flops 209844736 | bytes 25311440 | solution.py:46
  206.8 9.8 %while.71 = (s32[]{:T(128)}, f32[1024,32]{0,1:T(8,128)S(1)}, f32[1024,32]{0,1:T(8,128)S(1)}, f32[2,512,32]{1,2,0:T(8,128)}, bf16[2,512,32]{1,2,0:T(8,128)(2,1)S(...) while((s32[]{:T(128)}, f32[1024,32]{0,1:T(8,128)S(1)}, ...), condition=%wide.region_14.14_spmd.clone, body=%wide.region_10.13_spmd.clone.sunk | while | flops 209844736 | bytes 25311440 | solution.py:46
  222.1 9.7 %while.71 = (s32[]{:T(128)}, f32[1024,32]{0,1:T(8,128)S(1)}, f32[1024,32]{0,1:T(8,128)S(1)}, f32[2,512,32]{1,2,0:T(8,128)}, bf16[2,512,32]{1,2,0:T(8,128)(2,1)S(...) while((s32[]{:T(128)}, f32[1024,32]{0,1:T(8,128)S(1)}, ...), condition=%wide.region_14.14_spmd.clone, body=%wide.region_10.13_spmd.clone.sunk | while | flops 209844736 | bytes 25311440 | solution.py:46
  237.4 9.8 %while.71 = (s32[]{:T(128)}, f32[1024,32]{0,1:T(8,128)S(1)}, f32[1024,32]{0,1:T(8,128)S(1)}, f32[2,512,32]{1,2,0:T(8,128)}, bf16[2,512,32]{1,2,0:T(8,128)(2,1)S(...) while((s32[]{:T(128)}, f32[1024,32]{0,1:T(8,128)S(1)}, ...), condition=%wide.region_14.14_spmd.clone, body=%wide.region_10.13_spmd.clone.sunk | while | flops 209844736 | bytes 25311440 | solution.py:46
  250.6 4.5 copy.343
  255.1 3.3 reshape_reshape.33
  275.2 13.8 %all-to-all-start.2 = ((bf16[512,1,2,512]{3,2,1,0:T(2,128)(2,1)}), bf16[512,1,2,512]{3,2,1,0:T(2,128)(2,1)S(1)}, u32[]{:S(2)}, u32[]{:S(2)}) async-start(bf16[512,1,2,512]{3,2,1,0:T(2,128)(2,1)} %copy.286), calls=%async_computation.2 | async-start | bytes 2097152 | tf_op jit(solution)/shard_map/all_to_all | solution.py:185
  289.3 79.4 %psum.23 = f32[9,128]{1,0:T(8,128)S(1)} all-reduce(f32[9,128]{1,0:T(8,128)S(1)} %pad_maximum_fusion.7), channel_id=1, replica_groups=mesh['rows'=128,'batch'=2] {'rows','batch'}, use_global_device_ids=true, to_apply=%region_39.40 | all-reduce | flops 1152 | bytes 9216 | tf_op jit(solution)/shard_map/psum | solution.py:245
  380.0 2.8 fusion.80
  386.1 247.3 %all-reduce.7.cloned.1.call-done = (f32[128,384]{1,0:T(8,128)}, f32[128,128]{1,0:T(8,128)}) async-done(((f32[128,384]{1,0:T(8,128)}, f32[128,128]{1,0:T(8,128)}), (f32[128,384]{1,0:T(8,128)}, f32[128,128]{1,0:T(8,128)})) %all-reduce.7.cloned.1.call-update) | async-done | bytes 262160 | tf_op jit(solution)/shard_map/psum | solution.py:245
  (510 shorter events, 212.8 us)
Async XLA Ops:
  9.3 21.3 %copy-start.23 = (bf16[2048,64]{0,1:T(8,128)(2,1)}, bf16[2048,64]{0,1:T(8,128)(2,1)S(1)}, u32[]{:S(2)}) copy-start(bf16[2048,64]{0,1:T(8,128)(2,1)S(1)} %get-tuple-element.529) | copy-start | bytes 786436
  9.3 18.8 %copy-start.2 = (bf16[1,4,512,128]{3,2,1,0:T(8,128)(2,1)S(1)}, bf16[1,4,512,128]{3,2,1,0:T(8,128)(2,1)}, u32[]{:S(2)}) copy-start(bf16[1,4,512,128]{3,2,1,0:T(8,128)(2,1)} %param.13) | copy-start | bytes 1572868
  9.6 19.5 %copy-start.35 = (bf16[128,384]{1,0:T(8,128)(2,1)S(1)}, bf16[128,384]{1,0:T(8,128)(2,1)}, u32[]{:S(2)}) copy-start(bf16[128,384]{1,0:T(8,128)(2,1)} %param.15) | copy-start | bytes 294916
  10.8 102.8 %all-to-all-start.1 = ((bf16[4,128,2,128]{3,2,0,1:T(2,128)(2,1)}), bf16[4,128,2,128]{3,2,0,1:T(2,128)(2,1)}, u32[]{:S(2)}, u32[]{:S(2)}) async-start(bf16[4,128,2,128]{3,2,0,1:T(2,128)(2,1)} %copy.266), calls=%async_computation.1 | async-start | bytes 524288 | tf_op jit(solution)/shard_map/all_to_all | solution.py:159
  28.1 4.0 copy-start.21
  28.2 12.7 %copy-start.4 = (bf16[4,1024,32]{2,1,0:T(8,128)(2,1)}, bf16[4,1024,32]{2,1,0:T(8,128)(2,1)S(1)}, u32[]{:S(2)}) copy-start(bf16[4,1024,32]{2,1,0:T(8,128)(2,1)S(1)} %fusion.83) | copy-start | bytes 786436
  28.4 3.7 copy-start.40
  35.2 4.4 copy-start.30
  40.9 3.7 copy-start.7
  44.6 63.6 %copy-start.54 = (bf16[9,128]{1,0:T(8,128)(2,1)S(1)}, bf16[9,128]{1,0:T(8,128)(2,1)}, u32[]{:S(2)}) copy-start(bf16[9,128]{1,0:T(8,128)(2,1)} %param.17) | copy-start | bytes 6916
  105.8 4.4 copy-start.6
  105.8 3.4 copy-start.9
  105.8 3.4 copy-start.37
  105.8 3.4 copy-start.38
  113.5 16.3 %copy-start.28 = (f32[4,1024,32]{1,2,0:T(8,128)S(1)}, f32[4,1024,32]{1,2,0:T(8,128)}, u32[]{:S(2)}) copy-start(f32[4,1024,32]{1,2,0:T(8,128)} %get-tuple-element.210) | copy-start | bytes 1572868
  113.5 41.3 %all-to-all-start = ((bf16[4,128,2,384]{3,2,0,1:T(2,128)(2,1)}), bf16[4,128,2,384]{3,2,0,1:T(2,128)(2,1)}, u32[]{:S(2)}, u32[]{:S(2)}) async-start(bf16[4,128,2,384]{3,2,0,1:T(2,128)(2,1)} %copy.261), calls=%async_computation | async-start | bytes 1572864 | tf_op jit(solution)/shard_map/all_to_all | solution.py:158
  185.8 3.5 copy-start.5
  273.1 16.1 %copy-start.44 = (f32[9,64]{1,0:T(8,128)S(1)}, f32[9,64]{1,0:T(8,128)}, u32[]{:S(2)}) copy-start(f32[9,64]{1,0:T(8,128)} %stack.69) | copy-start | bytes 6916
  275.2 94.1 %all-to-all-start.2 = ((bf16[512,1,2,512]{3,2,1,0:T(2,128)(2,1)}), bf16[512,1,2,512]{3,2,1,0:T(2,128)(2,1)S(1)}, u32[]{:S(2)}, u32[]{:S(2)}) async-start(bf16[512,1,2,512]{3,2,1,0:T(2,128)(2,1)} %copy.286), calls=%async_computation.2 | async-start | bytes 2097152 | tf_op jit(solution)/shard_map/all_to_all | solution.py:185
  289.0 344.3 %all-reduce.7.cloned.1.call-start = ((), (), s32[]{:S(2)}) async-start(), calls=%async_computation.3 | async-start | bytes 524288 | tf_op jit(solution)/shard_map/psum | solution.py:245
  372.5 3.9 copy-start.11
  372.5 5.0 copy-start.27
  375.1 3.6 copy-start.10
  382.8 253.6 %copy-start.1 = (bf16[128,128]{1,0:T(8,128)(2,1)S(1)}, bf16[128,128]{1,0:T(8,128)(2,1)}, u32[]{:S(2)}) copy-start(bf16[128,128]{1,0:T(8,128)(2,1)} %param.16) | copy-start | bytes 98308
  (63 other events, 84.9 us)
Sparse Core Ops, SparseCore 0:
  384.2 249.1 all-reduce.6
where the time goes:
time: 649 us; the launch traced here: 644 us
  waiting for transfers between devices  247 us (38%)
  local copies, waits for them, and re-layouts  142 us (22%)
  blocking collectives  79.4 us (12%)
  matrix products  57.3 us (9%)
  other arithmetic  55.3 us (9%)
  starting transfers between devices  46 us (7%)
  between operations  15.5 us (2%)
    psum x1, waiting for transfers between devices, body(): lax.psum((grad_qkv_part, grad_proj_part, tap_total), ('rows', 'batch'))  247 us
    psum x1, blocking collectives, body(): lax.psum((grad_qkv_part, grad_proj_part, tap_total), ('rows', 'batch'))  79.4 us
    another operation x21, other arithmetic  22.5 us
    dynamic_update_slice x32, local copies, waits for them, and re-layouts, stripes_backward(): results = lax.map(lambda item_parts: stripe_head(*item_parts), pieces)  17.5 us
    all_to_all x1, starting transfers between devices, body(): lax.all_to_all(grad_vert, 'rows', split_axis=1, concat_axis=0, tiled=True)  17.2 us
    dot_general x16, matrix products, advance(): jnp.dot(grad_block, values.T, preferred_element_type=jnp.float32)  17.1 us
    all_to_all x1, starting transfers between devices, body(): lax.all_to_all(first_part, 'rows', split_axis=1, concat_axis=0, tiled=True)  14.9 us
    while x64, local copies, waits for them, and re-layouts  14.2 us
  transfers between devices with their start and end apart: 4, of which 1 were waited for; matrix products, arithmetic and copies ran while one was open for 16% of the time, Pallas kernels for 0%

commit v1 on v0

v1 whole, which is shorter than its diff:
```python
import functools

import jax
import jax.numpy as jnp
from jax import lax
from jax.experimental import pallas as pl
from jax.experimental.pallas import tpu as pltpu
from jax.sharding import PartitionSpec as P

NUM_HEADS = 4
STRIPE = 2
EPSILON = 1e-05
LOG2E = 1.4426950408889634
CONTRACT_COLS = (((1,), (1,)), ((), ()))
CONTRACT_ROWS = (((0,), (0,)), ((), ()))
MESH = pl.DeviceIdType.MESH
QUERY_BLOCK = 512


def dot(left, right, dims=(((1,), (0,)), ((), ()))):
    return lax.dot_general(left, right, dims, preferred_element_type=jnp.float32)


def normalise(tokens):
    centred = tokens - jnp.mean(tokens, axis=1, keepdims=True)
    inv_std = lax.rsqrt(jnp.mean(centred * centred, axis=1, keepdims=True) + EPSILON)
    return centred * inv_std, inv_std


def attention(nat, tra, outs, length, heads, size):
    out_ref, dq_ref, dk_ref, dv_ref = outs
    half = heads * size
    scale = size ** (-0.5)
    block = QUERY_BLOCK
    for step in range(length // block):
        rows = slice(step * block, (step + 1) * block)
        for head in range(heads):
            cols = [slice(part * half + head * size, part * half + (head + 1) * size) for part in range(4)]
            mine = slice(head * size, (head + 1) * size)
            k_tra = tra[cols[1], :]
            v_tra = tra[cols[2], :]
            scores = dot(nat[rows, cols[0]], k_tra)
            d_probs = dot(nat[rows, cols[3]], v_tra)
            row_max = jnp.max(scores, axis=1, keepdims=True)
            raised = jnp.exp2((scores - row_max) * (scale * LOG2E))
            probs = raised * (1.0 / jnp.sum(raised, axis=1, keepdims=True))
            probs_low = probs.astype(jnp.bfloat16)
            inner = jnp.sum(probs * d_probs, axis=1, keepdims=True)
            d_scores = (probs * (d_probs - inner) * scale).astype(jnp.bfloat16)
            out_ref[mine, rows] = dot(v_tra, probs_low, CONTRACT_COLS)
            dq_ref[mine, rows] = dot(k_tra, d_scores, CONTRACT_COLS)
            dv_part = dot(tra[cols[3], rows], probs_low)
            dk_part = dot(tra[cols[0], rows], d_scores)
            if step == 0:
                dv_ref[mine, :] = dv_part
                dk_ref[mine, :] = dk_part
            else:
                dv_ref[mine, :] += dv_part
                dk_ref[mine, :] += dk_part


def lepe(values, grads, taps, length, vertical):
    half = values.shape[0]
    lane = lax.broadcasted_iota(jnp.int32, (half, length), 1)
    if vertical:
        second = lax.rem(lane, 2) == 1
        apart, low, high = 2, lane < 2, lane >= length - 2

        def swap(source):
            return jnp.where(second, pltpu.roll(source, 1, 1), pltpu.roll(source, length - 1, 1))

        def tap(long_off, short_off):
            return 3 * (long_off + 1) + short_off + 1

    else:
        span = length // 2
        second = lane >= span
        place = lax.rem(lane, span)
        apart, low, high = 1, place == 0, place == span - 1

        def swap(source):
            return jnp.concatenate([source[:, span:], source[:, :span]], axis=1)

        def tap(long_off, short_off):
            return 3 * (short_off + 1) + long_off + 1

    def moved(source, long_off):
        if long_off == 0:
            return source
        if long_off > 0:
            return jnp.where(high, 0.0, pltpu.roll(source, length - apart, 1))
        return jnp.where(low, 0.0, pltpu.roll(source, apart, 1))

    def weight(index):
        return taps[:, index : index + 1]

    values_swap, grads_swap = swap(values), swap(grads)
    out = jnp.zeros((half, length), jnp.float32)
    d_values = jnp.zeros((half, length), jnp.float32)
    sums = [None] * 9
    for off in (-1, 0, 1):
        near, far = moved(values, off), moved(values_swap, off)
        out = out + weight(tap(off, 0)) * near
        out = out + jnp.where(second, weight(tap(off, -1)), weight(tap(off, 1))) * far
        d_values = d_values + weight(tap(off, 0)) * moved(grads, -off)
        d_values = d_values + jnp.where(second, weight(tap(off, 1)), weight(tap(off, -1))) * moved(grads_swap, -off)
        sums[tap(off, 0)] = jnp.sum(grads * near, axis=1, keepdims=True)
        cross = grads * far
        sums[tap(off, 1)] = jnp.sum(jnp.where(second, 0.0, cross), axis=1, keepdims=True)
        sums[tap(off, -1)] = jnp.sum(jnp.where(second, cross, 0.0), axis=1, keepdims=True)
    spot = lax.broadcasted_iota(jnp.int32, (half, 128), 1)
    tap_sums = jnp.zeros((half, 128), jnp.float32)
    for index in range(9):
        tap_sums = jnp.where(spot == index, sums[index], tap_sums)
    return out, d_values, tap_sums


def window(tokens, grads, w_nat, w_tra, w_out, taps, scratch, vertical):
    nat, tra, out_s, dq_s, dk_s, dv_s = scratch
    length = tokens.shape[0]
    half = w_out.shape[0]
    unit, _ = normalise(tokens)
    normed = unit.astype(jnp.bfloat16)
    nat[:, : 3 * half] = dot(normed, w_nat).astype(jnp.bfloat16)
    nat[:, 3 * half :] = dot(grads, w_out, CONTRACT_COLS).astype(jnp.bfloat16)
    tra[: 3 * half, :] = dot(w_tra, normed, CONTRACT_COLS).astype(jnp.bfloat16)
    tra[3 * half :, :] = dot(w_out, grads, CONTRACT_COLS).astype(jnp.bfloat16)
    heads = NUM_HEADS // 2
    attention(nat, tra, (out_s, dq_s, dk_s, dv_s), length, heads, half // heads)
    values = tra[2 * half : 3 * half, :].astype(jnp.float32)
    lifted = tra[3 * half :, :].astype(jnp.float32)
    near_out, near_dv, tap_sums = lepe(values, lifted, taps, length, vertical)
    attn = (out_s[...] + near_out).astype(jnp.bfloat16)
    grad_tokens = jnp.concatenate(
        [
            dq_s[...].astype(jnp.bfloat16),
            dk_s[...].astype(jnp.bfloat16),
            (dv_s[...] + near_dv).astype(jnp.bfloat16),
        ],
        axis=0,
    )
    return grad_tokens, dot(grad_tokens, normed), dot(attn, grads), tap_sums


def windows_kernel(vertical, x_ref, g_ref, wn_ref, wt_ref, wo_ref, tap_ref, gt_ref, qkv_ref, proj_ref, tap_out, *scratch):
    if vertical:
        length = x_ref.shape[0] * x_ref.shape[3]
        tokens = x_ref[:, 0, 0].astype(jnp.float32).reshape(length, x_ref.shape[4])
        grads = g_ref[:, 0, 0].astype(jnp.float32).reshape(length, x_ref.shape[4]).astype(jnp.bfloat16)
    else:
        tokens = x_ref[...].astype(jnp.float32)
        grads = g_ref[...]
    grad_tokens, qkv_part, proj_part, tap_part = window(
        tokens, grads, wn_ref[...], wt_ref[...], wo_ref[...], tap_ref[...], scratch, vertical
    )
    gt_ref[...] = grad_tokens.astype(jnp.float32).T.astype(jnp.bfloat16)

    @pl.when(pl.program_id(0) == 0)
    def _():
        qkv_ref[...] = qkv_part
        proj_ref[...] = proj_part
        tap_out[...] = tap_part

    @pl.when(pl.program_id(0) > 0)
    def _():
        qkv_ref[...] += qkv_part
        proj_ref[...] += proj_part
        tap_out[...] += tap_part


def run_windows(source_x, source_g, weights, vertical):
    w_nat, w_tra, w_out, taps = weights
    half = w_out.shape[0]
    channels = w_out.shape[1]
    if vertical:
        blocks, _, count, rows, _ = source_x.shape
        length = blocks * rows
        x_spec = pl.BlockSpec((blocks, 1, 1, rows, channels), lambda i: (0, 0, i, 0, 0))
        g_spec = pl.BlockSpec((blocks, 1, 1, rows, channels), lambda i: (0, 1, i, 0, 0))
    else:
        length = 1024
        count = source_x.shape[0] // length
        x_spec = pl.BlockSpec((length, channels), lambda i: (i, 0))
        g_spec = x_spec

    def whole(shape):
        return pl.BlockSpec(shape, lambda i: (0, 0))

    return pl.pallas_call(
        functools.partial(windows_kernel, vertical),
        grid=(count,),
        in_specs=[x_spec, g_spec] + [whole(w.shape) for w in weights],
        out_specs=[
            pl.BlockSpec((length, 3 * half), lambda i: (i, 0)),
            whole((3 * half, channels)),
            whole((half, channels)),
            whole((half, 128)),
        ],
        out_shape=[
            jax.ShapeDtypeStruct((count * length, 3 * half), jnp.bfloat16),
            jax.ShapeDtypeStruct((3 * half, channels), jnp.float32),
            jax.ShapeDtypeStruct((half, channels), jnp.float32),
            jax.ShapeDtypeStruct((half, 128), jnp.float32),
        ],
        scratch_shapes=[
            pltpu.VMEM((length, 4 * half), jnp.bfloat16),
            pltpu.VMEM((4 * half, length), jnp.bfloat16),
        ]
        + [pltpu.VMEM((half, length), jnp.float32)] * 4,
        compiler_params=pltpu.CompilerParams(vmem_limit_bytes=58 << 20),
        cost_estimate=pl.CostEstimate(flops=count * 3 * 10**9, bytes_accessed=4 << 20, transcendentals=count * 2 << 20),
    )(source_x, source_g, *weights)


def final_kernel(x_ref, g_ref, gh_ref, gv_ref, wh_ref, wv_ref, out_ref):
    unit, inv_std = normalise(x_ref[...].astype(jnp.float32))
    grad_unit = dot(gh_ref[...], wh_ref[...]) + dot(gv_ref[...], wv_ref[...])
    mean = jnp.mean(grad_unit, axis=1, keepdims=True)
    along = jnp.mean(grad_unit * unit, axis=1, keepdims=True)
    grad_norm = (grad_unit - mean - unit * along) * inv_std
    out_ref[...] = (g_ref[...].astype(jnp.float32) + grad_norm).astype(jnp.bfloat16)


def finish(tokens, grads, gt_h, gt_v, wt_h, wt_v):
    count, channels = tokens.shape
    block = min(count, 1024)
    row = pl.BlockSpec((block, channels), lambda i: (i, 0))
    wide = pl.BlockSpec((block, gt_h.shape[1]), lambda i: (i, 0))
    whole = pl.BlockSpec(wt_h.shape, lambda i: (0, 0))
    return pl.pallas_call(
        final_kernel,
        grid=(count // block,),
        in_specs=[row, row, wide, wide, whole, whole],
        out_specs=row,
        out_shape=jax.ShapeDtypeStruct((count, channels), jnp.bfloat16),
    )(tokens, grads, gt_h, gt_v, wt_h, wt_v)


PLANE = 32
DEPTH = 8


def reduce_kernel(parts, out, plane_buf, depth_buf, send_a, recv_a, send_b, recv_b, send_c, recv_c):
    row = lax.axis_index("rows")
    batch = lax.axis_index("batch")
    core = row % 2
    z_high = (row // 2) % 4
    mine = (row // 8) * 2 + core
    level = z_high * 2 + batch

    def plane_peer(other):
        return ((other // 2) * 8 + z_high * 2 + other % 2, batch)

    def depth_peer(other):
        return ((row // 8) * 8 + (other // 2) * 2 + core, other % 2)

    barrier = pltpu.get_barrier_semaphore()

    @pl.loop(1, PLANE)
    def _(step):
        pl.semaphore_signal(barrier, inc=1, device_id=plane_peer((mine + step) % PLANE), device_id_type=MESH)

    @pl.loop(1, DEPTH)
    def _(step):
        pl.semaphore_signal(barrier, inc=1, device_id=depth_peer((level + step) % DEPTH), device_id_type=MESH)

    pl.semaphore_wait(barrier, PLANE - 1 + DEPTH - 1)

    def copy_a(other, slot):
        return pltpu.make_async_remote_copy(
            src_ref=parts.at[other], dst_ref=plane_buf.at[slot], send_sem=send_a.at[other], recv_sem=recv_a.at[slot],
            device_id=plane_peer(other), device_id_type=MESH,
        )

    def copy_b(other, slot):
        return pltpu.make_async_remote_copy(
            src_ref=depth_buf.at[level], dst_ref=depth_buf.at[slot], send_sem=send_b.at[other], recv_sem=recv_b.at[slot],
            device_id=depth_peer(other), device_id_type=MESH,
        )

    def copy_c(other, slot):
        return pltpu.make_async_remote_copy(
            src_ref=out.at[mine], dst_ref=out.at[slot], send_sem=send_c.at[other], recv_sem=recv_c.at[slot],
            device_id=plane_peer(other), device_id_type=MESH,
        )

    @pl.loop(1, PLANE)
    def _(step):
        copy_a((mine + step) % PLANE, mine).start()

    plane_buf[mine] = parts[mine]

    @pl.loop(1, PLANE)
    def _(step):
        other = (mine + step) % PLANE
        copy_a(other, other).wait_recv()

    total = plane_buf[0]
    for index in range(1, PLANE):
        total = total + plane_buf[index]
    depth_buf[level] = total

    @pl.loop(1, DEPTH)
    def _(step):
        copy_b((level + step) % DEPTH, level).start()

    @pl.loop(1, DEPTH)
    def _(step):
        other = (level + step) % DEPTH
        copy_b(other, other).wait_recv()

    total = depth_buf[0]
    for index in range(1, DEPTH):
        total = total + depth_buf[index]
    out[mine] = total

    @pl.loop(1, PLANE)
    def _(step):
        copy_c((mine + step) % PLANE, mine).start()

    @pl.loop(1, PLANE)
    def _(step):
        other = (mine + step) % PLANE
        copy_c(other, other).wait_recv()

    @pl.loop(1, PLANE)
    def _(step):
        other = (mine + step) % PLANE
        copy_a(other, mine).wait_send()
        copy_c(other, mine).wait_send()

    @pl.loop(1, DEPTH)
    def _(step):
        copy_b((level + step) % DEPTH, level).wait_send()


def all_sum(parts):
    chunk = parts.shape[1:]
    vmem = pl.BlockSpec(memory_space=pltpu.VMEM)
    return pl.pallas_call(
        reduce_kernel,
        in_specs=[vmem],
        out_specs=vmem,
        out_shape=jax.ShapeDtypeStruct(parts.shape, jnp.float32),
        scratch_shapes=[
            pltpu.VMEM((PLANE,) + chunk, jnp.float32),
            pltpu.VMEM((DEPTH,) + chunk, jnp.float32),
            pltpu.SemaphoreType.DMA((PLANE,)),
            pltpu.SemaphoreType.DMA((PLANE,)),
            pltpu.SemaphoreType.DMA((DEPTH,)),
            pltpu.SemaphoreType.DMA((DEPTH,)),
            pltpu.SemaphoreType.DMA((PLANE,)),
            pltpu.SemaphoreType.DMA((PLANE,)),
        ],
        compiler_params=pltpu.CompilerParams(collective_id=0, has_side_effects=True),
    )(parts)


def body(features, grad_out, qkv_weight, proj_weight, lepe_weight):
    _, band_rows, map_cols, channels = features.shape
    half = channels // 2
    owners = lax.axis_size("rows")
    stripes = map_cols // owners // STRIPE
    tokens = features.reshape(-1, channels)
    grads = grad_out.reshape(-1, channels)

    def direction(first):
        w_nat = jnp.concatenate([qkv_weight[:, c + first : c + first + half] for c in (0, channels, 2 * channels)], axis=1)
        taps = lepe_weight[:, first : first + half].astype(jnp.float32).T
        return w_nat, w_nat.T, proj_weight[first : first + half], taps

    horiz, vert = direction(0), direction(half)

    def pack(source):
        split = source.reshape(band_rows, owners, stripes, STRIPE, channels).transpose(1, 2, 0, 3, 4)
        return split.reshape(owners, 1, stripes, band_rows * STRIPE, channels)

    sent = jnp.concatenate([pack(features), pack(grad_out)], axis=1)
    arrived = lax.all_to_all(sent, "rows", split_axis=0, concat_axis=0, tiled=True)
    gt_h, qkv_h, proj_h, tap_h = run_windows(tokens, grads, horiz, False)
    gt_v, qkv_v, proj_v, tap_v = run_windows(arrived, arrived, vert, True)
    back = gt_v.reshape(stripes, owners, band_rows * STRIPE, 3 * half).transpose(1, 0, 2, 3)
    returned = lax.all_to_all(back, "rows", split_axis=0, concat_axis=0, tiled=True)
    returned = returned.reshape(owners, stripes, band_rows, STRIPE, 3 * half).transpose(2, 0, 1, 3, 4)
    grad_features = finish(tokens, grads, gt_h, returned.reshape(-1, 3 * half), horiz[1], vert[1])

    tap_rows = jnp.concatenate([tap_h[:, :9], tap_v[:, :9]], axis=0).T
    main = jnp.concatenate([qkv_h, qkv_v, proj_h, proj_v], axis=0).reshape(PLANE, -1, channels)
    extra = jnp.pad(tap_rows, ((0, PLANE - 9), (0, 0))).reshape(PLANE, 1, channels)
    summed = all_sum(jnp.concatenate([main, extra], axis=1))
    total_tokens = lax.axis_size("batch") * owners * band_rows * map_cols
    summed = summed * total_tokens ** (-0.5)
    flat = summed[:, :-1].reshape(-1, channels)
    h_rows, v_rows = flat[: 3 * half], flat[3 * half : 6 * half]
    grad_qkv = jnp.concatenate(
        [piece[part * half : (part + 1) * half] for part in range(3) for piece in (h_rows, v_rows)], axis=0
    ).T
    return (
        grad_features.reshape(features.shape),
        grad_qkv,
        flat[6 * half :],
        summed[:9, -1],
    )


def solution(mesh):
    in_specs = (P("batch", "rows", None, None), P("batch", "rows", None, None), P(), P(), P())
    out_specs = (P("batch", "rows", None, None), P(), P(), P())
    return jax.shard_map(body, mesh=mesh, in_specs=in_specs, out_specs=out_specs, check_vma=False)
```

time: 649 us -> 145 us (0.22)
  waiting for transfers between devices: 247 us -> 26.6 us
  local copies, waits for them, and re-layouts: 142 us -> 16.2 us
  blocking collectives: 79.4 us -> 0 us
  Pallas kernels: 0 us -> 71.8 us
  matrix products: 57.3 us -> 0 us
  other arithmetic: 55.3 us -> 5.44 us
  starting transfers between devices: 46 us -> 23.2 us
  between operations: 15.5 us -> 0.91 us
    psum x1 -> x0, waiting for transfers between devices: 247 us -> none  [body(): lax.psum((grad_qkv_part, grad_proj_part, tap_total), ('rows', 'batch'))]
    psum x1 -> x0, blocking collectives: 79.4 us -> none  [body(): lax.psum((grad_qkv_part, grad_proj_part, tap_total), ('rows', 'batch'))]
    pallas_call x0 -> x4, Pallas kernels: none -> 71.8 us  [the longest x2 39.3 us: run_windows(): pl.pallas_call(functools.partial(windows_kernel, vertical), grid=(count,)...]
    dot_general x102 -> x0, matrix products: 57.3 us -> none  [the longest x16 17.1 us: advance(): jnp.dot(grad_block, values.T, preferred_element_type=jnp.float32)]
    while x83 -> x0, local copies, waits for them, and re-layouts: 27.7 us -> none
    all_to_all x3 -> x2, waiting for transfers between devices: 0.01 us -> 26.6 us  [the longest x1 26.6 us: body(): lax.all_to_all(sent, 'rows', split_axis=0, concat_axis=0, tiled=True)]
    another operation x21 -> x0, local copies, waits for them, and re-layouts: 25.4 us -> none
    reshape x24 -> x4, local copies, waits for them, and re-layouts: 29.2 us -> 5.92 us  [the longest x1 2.29 us: body(): gt_v.reshape(stripes, owners, band_rows * STRIPE, 3 * half)]
  transfers between devices with their start and end apart: 4 -> 2, of which waited for: 1 -> 1; matrix products, arithmetic and copies ran while one was open for 16% -> 8% of each run, Pallas kernels for 0% -> 34%
where the time goes in v1:
time: 145 us; the launch traced here: 144 us
  Pallas kernels  71.8 us (50%)
  waiting for transfers between devices  26.6 us (18%)
  starting transfers between devices  23.2 us (16%)
  local copies, waits for them, and re-layouts  16.2 us (11%)
  other arithmetic  5.44 us (4%)
    pallas_call x2, Pallas kernels, run_windows(): pl.pallas_call(functools.partial(windows_kernel, vertical), grid=(count,)...  39.3 us
    pallas_call x1, Pallas kernels, all_sum(): pl.pallas_call(reduce_kernel, in_specs=[vmem], out_specs=vmem, out_shape=...  29 us
    all_to_all x1, waiting for transfers between devices, body(): lax.all_to_all(sent, 'rows', split_axis=0, concat_axis=0, tiled=True)  26.6 us
    all_to_all x1, starting transfers between devices, body(): lax.all_to_all(sent, 'rows', split_axis=0, concat_axis=0, tiled=True)  16.5 us
    all_to_all x1, starting transfers between devices, body(): lax.all_to_all(back, 'rows', split_axis=0, concat_axis=0, tiled=True)  6.72 us
    pallas_call x1, Pallas kernels, finish(): pl.pallas_call(final_kernel, grid=(count // block,), in_specs=[row, row,...  3.55 us
    unnamed x29, local copies, waits for them, and re-layouts  3.22 us
  transfers between devices with their start and end apart: 2, of which 1 were waited for; matrix products, arithmetic and copies ran while one was open for 8% of the time, Pallas kernels for 34%

profile of v1, /device:TPU:1, one launch (start us, length us, event | category | flops | bytes accessed | tf_op | source)
XLA Modules:
  0.0 144.3 jit_solution(830895936726204120)
XLA Ops:
  0.6 1.5 %copy.57 = bf16[4,128,2,2,128]{4,3,0,2,1:T(2,128)(2,1)S(1)} copy(bf16[4,128,2,2,128]{4,3,2,1,0:T(2,128)(2,1)} %bitcast.45) | data formatting | bytes 1048576 | tf_op jit(solution)/shard_map/reshape | solution.py:375
  2.5 1.1 pad_maximum_fusion
  3.6 16.5 %all-to-all-start = ((bf16[128,2,2,8,128]{4,3,2,1,0:T(8,128)(2,1)}), bf16[128,2,2,8,128]{4,3,2,1,0:T(8,128)(2,1)S(1)}, u32[]{:S(2)}, u32[]{:S(2)}) async-start(bf16[128,2,2,8,128]{4,3,2,1,0:T(8,128)(2,1)} %pad_maximum_fusion), calls=%async_computation | async-start | bytes 2097152 | tf_op jit(solution)/shard_map/all_to_all | solution.py:379
  21.1 0.6 fusion
  21.7 0.7 copy.62.wn_ref
  22.5 0.6 fusion.1
  23.1 0.7 copy.55.wn_ref
  25.2 26.6 %all-to-all-done.x_ref.g_ref = bf16[128,2,2,8,128]{4,3,2,1,0:T(8,128)(2,1)S(1)} async-done(((bf16[128,2,2,8,128]{4,3,2,1,0:T(8,128)(2,1)}), bf16[128,2,2,8,128]{4,3,2,1,0:T(8,128)(2,1)S(1)}, u32[]{:S(2)}, u32[]{:S(2)}) %all-to-all-start) | async-done | bytes 1048608 | tf_op jit(solution)/shard_map/all_to_all | solution.py:379
  51.9 1.0 copy-done.1
  52.8 19.8 %shard_map.85 = (bf16[2048,192]{1,0:T(8,128)(2,1)}, f32[192,128]{1,0:T(8,128)}, f32[64,128]{1,0:T(8,128)}, f32[64,128]{1,0:T(8,128)}) custom-call(bf16[128,2,2,8,128]{4,3,2,1,0:T(8,128)(2,1)} %copy-done.1, bf16[128,2,2,8,128]{4,3,2,1,0:T(8,128)(2,1)} %copy-done.1, bf16[128,192]{1,0:T(8,128)(2,1)} %copy.62.wn_ref, ...), custom_call_target="tpu_custom_call" | custom-call | flops 6000000000 | bytes 4194304 | tf_op jit(solution)/shard_map/pallas_call | solution.py:189
  72.7 2.3 %copy.85 = bf16[2,128,8,192]{3,2,0,1:T(8,128)(2,1)} copy(bf16[2,128,8,192]{3,2,1,0:T(8,128)(2,1)} %bitcast.50) | data formatting | bytes 1572864 | tf_op jit(solution)/shard_map/reshape | solution.py:382
  75.0 6.7 %all-to-all-start.1 = ((bf16[128,2,8,192]{3,2,1,0:T(8,128)(2,1)}), bf16[128,2,8,192]{3,2,1,0:T(8,128)(2,1)S(1)}, u32[]{:S(2)}, u32[]{:S(2)}) async-start(bf16[128,2,8,192]{3,2,1,0:T(8,128)(2,1)} %bitcast.39), calls=%async_computation.1 | async-start | bytes 2097152 | tf_op jit(solution)/shard_map/all_to_all | solution.py:383
  82.3 19.4 %shard_map.84 = (bf16[2048,192]{1,0:T(8,128)(2,1)}, f32[192,128]{1,0:T(8,128)}, f32[64,128]{1,0:T(8,128)}, f32[64,128]{1,0:T(8,128)}) custom-call(bf16[2048,128]{1,0:T(8,128)(2,1)} %bitcast.42, bf16[2048,128]{1,0:T(8,128)(2,1)} %bitcast.46, bf16[128,192]{1,0:T(8,128)(2,1)} %copy.55.wn_ref, bf16[192,128]{1,0:T(8,128)(2,1)} %get-tuple-element.34.wt_ref.wh_ref, ...), custom_call_target="tpu_custom_call" | custom-call | flops 6000000000 | bytes 4194304 | tf_op jit(solution)/shard_map/pallas_call | solution.py:189
  101.8 0.9 copy.66
  102.9 0.7 copy-done.3
  103.6 0.8 pad_maximum_fusion.1.parts
  104.4 29.0 %shard_map.87 = f32[32,17,128]{2,1,0:T(8,128)} custom-call(f32[32,17,128]{2,1,0:T(8,128)} %pad_maximum_fusion.1.parts), custom_call_target="tpu_custom_call" | custom-call | tf_op jit(solution)/shard_map/pallas_call | solution.py:340
  133.4 1.0 broadcast_multiply_fusion
  134.4 0.6 slice.130
  136.3 0.8 concatenate.27
  137.1 1.0 copy.64
  138.1 0.8 copy.65
  138.9 1.8 %reshape.62.gv_ref = bf16[2048,192]{1,0:T(8,128)(2,1)} reshape(bf16[4,128,2,2,192]{4,3,2,1,0:T(2,128)(2,1)S(1)} %copy.65) | data formatting | bytes 1572864 | tf_op jit(solution)/shard_map/reshape | solution.py:385
  140.7 3.5 %shard_map.86 = bf16[2048,128]{1,0:T(8,128)(2,1)} custom-call(bf16[2048,128]{1,0:T(8,128)(2,1)} %bitcast.43, bf16[2048,128]{1,0:T(8,128)(2,1)} %bitcast.47, bf16[2048,192]{1,0:T(8,128)(2,1)} %get-tuple-element.12.gh_ref, bf16[2048,192]{1,0:T(8,128)(2,1)} %reshape.62.gv_ref, bf16[192,128]{1,0:T(8,128)(2,1)} %get-tuple-element.34.wt_ref.wh_ref, ...), custom_call_target="tpu_custom_call" | custom-call | tf_op jit(solution)/shard_map/pallas_call | solution.py:230
  (48 shorter events, 4.7 us)
Async XLA Ops:
  0.6 1.5 %copy-start = (bf16[1,4,512,128]{3,2,1,0:T(8,128)(2,1)S(1)}, bf16[1,4,512,128]{3,2,1,0:T(8,128)(2,1)}, u32[]{:S(2)}) copy-start(bf16[1,4,512,128]{3,2,1,0:T(8,128)(2,1)} %param.5) | copy-start | bytes 1572868
  3.6 16.5 %copy-start.9 = (bf16[9,128]{1,0:T(8,128)(2,1)S(1)}, bf16[9,128]{1,0:T(8,128)(2,1)}, u32[]{:S(2)}) copy-start(bf16[9,128]{1,0:T(8,128)(2,1)} %param.9) | copy-start | bytes 6916
  3.6 16.8 %copy-start.2 = (bf16[128,384]{1,0:T(8,128)(2,1)S(1)}, bf16[128,384]{1,0:T(8,128)(2,1)}, u32[]{:S(2)}) copy-start(bf16[128,384]{1,0:T(8,128)(2,1)} %param.7) | copy-start | bytes 294916
  3.6 48.3 %all-to-all-start = ((bf16[128,2,2,8,128]{4,3,2,1,0:T(8,128)(2,1)}), bf16[128,2,2,8,128]{4,3,2,1,0:T(8,128)(2,1)S(1)}, u32[]{:S(2)}, u32[]{:S(2)}) async-start(bf16[128,2,2,8,128]{4,3,2,1,0:T(8,128)(2,1)} %pad_maximum_fusion), calls=%async_computation | async-start | bytes 2097152 | tf_op jit(solution)/shard_map/all_to_all | solution.py:379
  23.8 0.8 copy-start.8
  51.9 1.0 copy-start.1
  75.0 62.1 %all-to-all-start.1 = ((bf16[128,2,8,192]{3,2,1,0:T(8,128)(2,1)}), bf16[128,2,8,192]{3,2,1,0:T(8,128)(2,1)S(1)}, u32[]{:S(2)}, u32[]{:S(2)}) async-start(bf16[128,2,8,192]{3,2,1,0:T(8,128)(2,1)} %bitcast.39), calls=%async_computation.1 | async-start | bytes 2097152 | tf_op jit(solution)/shard_map/all_to_all | solution.py:383
  82.3 20.4 %copy-start.6 = (f32[64,128]{1,0:T(8,128)S(1)}, f32[64,128]{1,0:T(8,128)}, u32[]{:S(2)}) copy-start(f32[64,128]{1,0:T(8,128)} %get-tuple-element.19) | copy-start | bytes 98308
  101.8 1.1 copy-start.4
  102.7 0.9 copy-start.3
  102.8 0.8 copy-start.7
  102.8 0.8 copy-start.5

commit v2 on v1

v2 whole, which is shorter than its diff:
```python
import jax
import jax.numpy as jnp
from jax import lax
from jax.experimental import pallas as pl
from jax.experimental.pallas import tpu as pltpu
from jax.sharding import PartitionSpec as P

NUM_HEADS = 4
STRIPE = 2
EPSILON = 1e-05
LOG2E = 1.4426950408889634
COLS = (((1,), (1,)), ((), ()))
ROWS = (((0,), (0,)), ((), ()))
MESH = pl.DeviceIdType.MESH
QUERY_BLOCK = 512
CH = 128
SIZE = 32
LEN = 1024
BAND = 4
WIDTH = 512
OWNERS = 128
PLANE = 32
DEPTH = 8
PIECE = 64
SCALE = SIZE ** (-0.5)


def dot(left, right, dims=(((1,), (0,)), ((), ()))):
    return lax.dot_general(left, right, dims, preferred_element_type=jnp.float32)


def normalise(tokens):
    centred = tokens - jnp.mean(tokens, axis=1, keepdims=True)
    inv_std = lax.rsqrt(jnp.mean(centred * centred, axis=1, keepdims=True) + EPSILON)
    return centred * inv_std, inv_std


def attention(nat, tra, out_s, dq_s, dk_s, dv_s):
    k_tra = tra[SIZE : 2 * SIZE, :]
    v_tra = tra[2 * SIZE : 3 * SIZE, :]
    for step in range(LEN // QUERY_BLOCK):
        rows = slice(step * QUERY_BLOCK, (step + 1) * QUERY_BLOCK)
        scores = dot(nat[rows, :SIZE], k_tra)
        d_probs = dot(nat[rows, 3 * SIZE :], v_tra)
        row_max = jnp.max(scores, axis=1, keepdims=True)
        raised = jnp.exp2((scores - row_max) * (SCALE * LOG2E))
        probs = raised * (1.0 / jnp.sum(raised, axis=1, keepdims=True))
        probs_low = probs.astype(jnp.bfloat16)
        inner = jnp.sum(probs * d_probs, axis=1, keepdims=True)
        d_scores = (probs * (d_probs - inner) * SCALE).astype(jnp.bfloat16)
        out_s[:, rows] = dot(v_tra, probs_low, COLS)
        dq_s[:, rows] = dot(k_tra, d_scores, COLS)
        dv_part = dot(tra[3 * SIZE :, rows], probs_low)
        dk_part = dot(tra[:SIZE, rows], d_scores)
        if step == 0:
            dv_s[...] = dv_part
            dk_s[...] = dk_part
        else:
            dv_s[...] += dv_part
            dk_s[...] += dk_part


def lepe(values, grads, taps, vertical):
    lane = lax.broadcasted_iota(jnp.int32, (SIZE, LEN), 1)
    if vertical:
        second = lane % 2 == 1
        apart, low, high = 2, lane < 2, lane >= LEN - 2

        def swap(source):
            return jnp.where(second, pltpu.roll(source, 1, 1), pltpu.roll(source, LEN - 1, 1))

        def tap(long_off, short_off):
            return 3 * (long_off + 1) + short_off + 1

    else:
        span = LEN // 2
        second = lane >= span
        place = lane % span
        apart, low, high = 1, place == 0, place == span - 1

        def swap(source):
            return jnp.concatenate([source[:, span:], source[:, :span]], axis=1)

        def tap(long_off, short_off):
            return 3 * (short_off + 1) + long_off + 1

    def moved(source, long_off):
        if long_off == 0:
            return source
        if long_off > 0:
            return jnp.where(high, 0.0, pltpu.roll(source, LEN - apart, 1))
        return jnp.where(low, 0.0, pltpu.roll(source, apart, 1))

    def weight(index):
        return taps[:, index : index + 1]

    values_swap, grads_swap = swap(values), swap(grads)
    out = jnp.zeros((SIZE, LEN), jnp.float32)
    d_values = jnp.zeros((SIZE, LEN), jnp.float32)
    sums = [None] * 9
    for off in (-1, 0, 1):
        near, far = moved(values, off), moved(values_swap, off)
        out = out + weight(tap(off, 0)) * near
        out = out + jnp.where(second, weight(tap(off, -1)), weight(tap(off, 1))) * far
        d_values = d_values + weight(tap(off, 0)) * moved(grads, -off)
        d_values = d_values + jnp.where(second, weight(tap(off, 1)), weight(tap(off, -1))) * moved(grads_swap, -off)
        sums[tap(off, 0)] = jnp.sum(grads * near, axis=1, keepdims=True)
        cross = grads * far
        sums[tap(off, 1)] = jnp.sum(jnp.where(second, 0.0, cross), axis=1, keepdims=True)
        sums[tap(off, -1)] = jnp.sum(jnp.where(second, cross, 0.0), axis=1, keepdims=True)
    spot = lax.broadcasted_iota(jnp.int32, (SIZE, CH), 1)
    tap_sums = jnp.zeros((SIZE, CH), jnp.float32)
    for index in range(9):
        tap_sums = jnp.where(spot == index, sums[index], tap_sums)
    return out, d_values, tap_sums


def kernel(
    x_ref, g_ref, qkv_ref, proj_ref, lepe_ref,
    gf_out, qkv_out, proj_out, lepe_out,
    w_tra, taps, sent, arrived, back, returned, pair, nat, tra, out_s, dq_s, dk_s, dv_s, unit_h, acc, tap_acc,
    parts, plane_buf, depth_buf, total,
    send_f, recv_f, send_r, recv_r, send_a, recv_a, send_b, recv_b, send_c, recv_c,
):
    row = lax.axis_index("rows")
    batch = lax.axis_index("batch")
    core = row % 2
    z_high = (row // 2) % 4
    mine = (row // 8) * 2 + core
    level = z_high * 2 + batch

    def plane_peer(other):
        return ((other // 2) * 8 + z_high * 2 + other % 2, batch)

    def depth_peer(other):
        return ((row // 8) * 8 + (other // 2) * 2 + core, other % 2)

    barrier = pltpu.get_barrier_semaphore()

    @pl.loop(1, OWNERS)
    def _(step):
        pl.semaphore_signal(barrier, inc=1, device_id=((row + step) % OWNERS, batch), device_id_type=MESH)

    @pl.loop(0, 4)
    def _(step):
        pl.semaphore_signal(barrier, inc=1, device_id=depth_peer(step * 2 + 1 - batch), device_id_type=MESH)

    out_row = lax.broadcasted_iota(jnp.int32, (256, 256), 0)
    in_row = lax.broadcasted_iota(jnp.int32, (256, 256), 1)
    source_row = ((out_row // 2) % 4) * PIECE + ((out_row // 8) % 16) * 4 + (out_row // 128) * 2 + out_row % 2
    permute = (in_row == source_row).astype(jnp.float32).astype(jnp.bfloat16)
    for q in range(WIDTH // PIECE):
        both = jnp.concatenate(
            [
                jnp.concatenate(
                    [ref[r * WIDTH + q * PIECE : r * WIDTH + (q + 1) * PIECE, :] for r in range(BAND)], axis=0
                )
                for ref in (x_ref, g_ref)
            ],
            axis=1,
        )
        packed = dot(permute, both).reshape(2, 16, 8, 2 * CH).astype(jnp.bfloat16)
        sent[0, q * 16 : (q + 1) * 16] = packed[0]
        sent[1, q * 16 : (q + 1) * 16] = packed[1]

    qkv_tra = qkv_ref[...].astype(jnp.float32).T
    for head in range(NUM_HEADS):
        rows = [qkv_tra[part * CH + head * SIZE : part * CH + (head + 1) * SIZE, :] for part in range(3)]
        rows.append(jnp.zeros((SIZE, CH), jnp.float32))
        w_tra[head, :, :CH] = jnp.concatenate(rows, axis=0).astype(jnp.bfloat16)
        w_tra[head, : 3 * SIZE, CH:] = jnp.zeros((3 * SIZE, CH), jnp.bfloat16)
        w_tra[head, 3 * SIZE :, CH:] = proj_ref[head * SIZE : (head + 1) * SIZE, :]
    taps[...] = jnp.concatenate([lepe_ref[...].astype(jnp.float32), jnp.zeros((7, CH), jnp.float32)], axis=0).T
    acc[...] = jnp.zeros_like(acc)
    tap_acc[...] = jnp.zeros_like(tap_acc)

    pl.semaphore_wait(barrier, OWNERS - 1 + 4)

    def forward(stripe, other, slot):
        return pltpu.make_async_remote_copy(
            src_ref=sent.at[stripe, other], dst_ref=arrived.at[stripe, slot],
            send_sem=send_f.at[stripe], recv_sem=recv_f.at[stripe],
            device_id=(other, batch), device_id_type=MESH,
        )

    def backward(stripe, head, other, slot):
        return pltpu.make_async_remote_copy(
            src_ref=back.at[stripe, head, other], dst_ref=returned.at[stripe, head, slot],
            send_sem=send_r.at[stripe, head], recv_sem=recv_r.at[stripe, head],
            device_id=(other, batch), device_id_type=MESH,
        )

    def all_forward(stripe):
        return pltpu.make_async_remote_copy(
            src_ref=sent.at[stripe, pl.ds(0, OWNERS - 1)], dst_ref=arrived.at[stripe, pl.ds(0, OWNERS - 1)],
            send_sem=send_f.at[stripe], recv_sem=recv_f.at[stripe],
            device_id=((row + 1) % OWNERS, batch), device_id_type=MESH,
        )

    def all_backward(stripe, head):
        return pltpu.make_async_remote_copy(
            src_ref=back.at[stripe, head, pl.ds(0, OWNERS - 1)], dst_ref=returned.at[stripe, head, pl.ds(0, OWNERS - 1)],
            send_sem=send_r.at[stripe, head], recv_sem=recv_r.at[stripe, head],
            device_id=((row + 1) % OWNERS, batch), device_id_type=MESH,
        )

    for stripe in range(2):

        @pl.loop(1, OWNERS)
        def _(step):
            forward(stripe, (row + step) % OWNERS, row).start()

    for stripe in range(2):
        arrived[stripe, row] = sent[stripe, row]

    def one_head(head, vertical):
        nat[...] = dot(pair[...], w_tra[head], COLS).astype(jnp.bfloat16)
        tra[...] = dot(w_tra[head], pair[...], COLS).astype(jnp.bfloat16)
        attention(nat, tra, out_s, dq_s, dk_s, dv_s)
        values = tra[2 * SIZE : 3 * SIZE, :].astype(jnp.float32)
        lifted = tra[3 * SIZE :, :].astype(jnp.float32)
        channels = slice(head * SIZE, (head + 1) * SIZE)
        near_out, near_dv, tap_sums = lepe(values, lifted, taps[channels, :], vertical)
        whole = jnp.concatenate(
            [
                dq_s[...].astype(jnp.bfloat16),
                dk_s[...].astype(jnp.bfloat16),
                (dv_s[...] + near_dv).astype(jnp.bfloat16),
                (out_s[...] + near_out).astype(jnp.bfloat16),
            ],
            axis=0,
        )
        tap_acc[channels, :] += tap_sums
        part = dot(whole, pair[...])
        acc[head, : 3 * SIZE, :] += part[: 3 * SIZE, :CH]
        acc[head, 3 * SIZE :, :] += part[3 * SIZE :, CH:]
        return whole

    @pl.loop(0, 2)
    def _(turn):
        base = pl.multiple_of(turn * LEN, LEN)
        unit, _ = normalise(x_ref[pl.ds(base, LEN), :].astype(jnp.float32))
        pair[:, :CH] = unit.astype(jnp.bfloat16)
        pair[:, CH:] = g_ref[pl.ds(base, LEN), :]
        for head in range(2):
            whole = one_head(head, False)
            share = dot(whole, w_tra[head, :, :CH], ROWS)
            if head == 0:
                unit_h[pl.ds(base, LEN), :] = share
            else:
                unit_h[pl.ds(base, LEN), :] += share

        all_forward(turn).wait_recv()
        unit, _ = normalise(arrived[turn, :, :, :CH].astype(jnp.float32).reshape(LEN, CH))
        pair[:, :CH] = unit.astype(jnp.bfloat16)
        pair[:, CH:] = arrived[turn, :, :, CH:].astype(jnp.float32).reshape(LEN, CH).astype(jnp.bfloat16)
        for head in range(2):
            whole = one_head(2 + head, True)
            back[turn, head] = whole.astype(jnp.float32).T.reshape(OWNERS, 8, CH).astype(jnp.bfloat16)

            @pl.loop(1, OWNERS)
            def _(step):
                backward(turn, head, (row + step) % OWNERS, row).start()

            returned[turn, head, row] = back[turn, head, row]

    tap_rows = tap_acc[...].T
    for index in range(PLANE):
        head, place = index // 8, index % 8
        parts[index, :16, :] = acc[head, place * 16 : (place + 1) * 16, :]
        if index < 9:
            parts[index, 16:, :] = tap_rows[index : index + 1, :]
        else:
            parts[index, 16:, :] = jnp.zeros((1, CH), jnp.float32)

    def copy_a(other, slot):
        return pltpu.make_async_remote_copy(
            src_ref=parts.at[other], dst_ref=plane_buf.at[slot], send_sem=send_a.at[other], recv_sem=recv_a.at[slot],
            device_id=plane_peer(other), device_id_type=MESH,
        )

    def copy_b(other, slot):
        return pltpu.make_async_remote_copy(
            src_ref=depth_buf.at[level], dst_ref=depth_buf.at[slot], send_sem=send_b.at[other], recv_sem=recv_b.at[slot],
            device_id=depth_peer(other), device_id_type=MESH,
        )

    def copy_c(other, slot):
        return pltpu.make_async_remote_copy(
            src_ref=total.at[mine], dst_ref=total.at[slot], send_sem=send_c.at[other], recv_sem=recv_c.at[slot],
            device_id=plane_peer(other), device_id_type=MESH,
        )

    @pl.loop(1, PLANE)
    def _(step):
        copy_a((mine + step) % PLANE, mine).start()

    plane_buf[mine] = parts[mine]

    @pl.loop(1, PLANE)
    def _(step):
        other = (mine + step) % PLANE
        copy_a(other, other).wait_recv()

    sum_a = plane_buf[0]
    for index in range(1, PLANE):
        sum_a = sum_a + plane_buf[index]
    depth_buf[level] = sum_a

    @pl.loop(1, DEPTH)
    def _(step):
        copy_b((level + step) % DEPTH, level).start()

    @pl.loop(1, DEPTH)
    def _(step):
        other = (level + step) % DEPTH
        copy_b(other, other).wait_recv()

    sum_b = depth_buf[0]
    for index in range(1, DEPTH):
        sum_b = sum_b + depth_buf[index]
    total[mine] = sum_b

    @pl.loop(1, PLANE)
    def _(step):
        copy_c((mine + step) % PLANE, mine).start()

    for stripe in range(2):
        for head in range(2):
            all_backward(stripe, head).wait_recv()

    @pl.loop(0, WIDTH // PIECE)
    def _(q):
        owners = pl.ds(q * 16, 16)
        grads = jnp.concatenate(
            [
                jnp.concatenate(
                    [returned[j, head, owners].astype(jnp.float32).reshape(128, CH) for j in range(2)], axis=0
                ).astype(jnp.bfloat16)
                for head in range(2)
            ],
            axis=1,
        )
        ordered = dot(permute, grads, ROWS).astype(jnp.bfloat16)
        weights = jnp.concatenate([w_tra[2, :, :CH], w_tra[3, :, :CH]], axis=0)
        grad_v = dot(ordered, weights)
        for r in range(BAND):
            place = pl.ds(pl.multiple_of(r * WIDTH + q * PIECE, PIECE), PIECE)
            unit, inv_std = normalise(x_ref[place, :].astype(jnp.float32))
            grad_unit = unit_h[place, :] + grad_v[r * PIECE : (r + 1) * PIECE, :]
            mean = jnp.mean(grad_unit, axis=1, keepdims=True)
            along = jnp.mean(grad_unit * unit, axis=1, keepdims=True)
            grad_norm = (grad_unit - mean - unit * along) * inv_std
            gf_out[place, :] = (g_ref[place, :].astype(jnp.float32) + grad_norm).astype(jnp.bfloat16)

    @pl.loop(1, PLANE)
    def _(step):
        other = (mine + step) % PLANE
        copy_c(other, other).wait_recv()

    z = (2 * 512 * 512) ** (-0.5)

    def rows_of(head, start):
        return [total[head * 8 + (start + half * 16) // 16, :16, :] for half in range(2)]

    for part in range(3):
        pieces = [piece for head in range(NUM_HEADS) for piece in rows_of(head, part * SIZE)]
        qkv_out[:, part * CH : (part + 1) * CH] = jnp.concatenate(pieces, axis=0).T * z
    proj_out[...] = jnp.concatenate([piece for head in range(NUM_HEADS) for piece in rows_of(head, 3 * SIZE)], axis=0) * z
    lepe_out[...] = jnp.concatenate([total[index, 16:, :] for index in range(9)], axis=0) * z

    for stripe in range(2):
        all_forward(stripe).wait_send()
        for head in range(2):
            all_backward(stripe, head).wait_send()

    @pl.loop(1, PLANE)
    def _(step):
        other = (mine + step) % PLANE
        copy_a(other, mine).wait_send()
        copy_c(other, mine).wait_send()

    @pl.loop(1, DEPTH)
    def _(step):
        copy_b((level + step) % DEPTH, level).wait_send()


def body(features, grad_out, qkv_weight, proj_weight, lepe_weight):
    tokens = BAND * WIDTH
    vmem = pl.BlockSpec(memory_space=pltpu.VMEM)
    low, wide = jnp.bfloat16, jnp.float32
    dma = pltpu.SemaphoreType.DMA
    grad_features, grad_qkv, grad_proj, grad_lepe = pl.pallas_call(
        kernel,
        in_specs=[vmem] * 5,
        out_specs=[vmem] * 4,
        out_shape=[
            jax.ShapeDtypeStruct((tokens, CH), low),
            jax.ShapeDtypeStruct((CH, 3 * CH), wide),
            jax.ShapeDtypeStruct((CH, CH), wide),
            jax.ShapeDtypeStruct((9, CH), wide),
        ],
        scratch_shapes=[
            pltpu.VMEM((NUM_HEADS, CH, 2 * CH), low),
            pltpu.VMEM((CH, 16), wide),
            pltpu.VMEM((2, OWNERS, 8, 2 * CH), low),
            pltpu.VMEM((2, OWNERS, 8, 2 * CH), low),
            pltpu.VMEM((2, 2, OWNERS, 8, CH), low),
            pltpu.VMEM((2, 2, OWNERS, 8, CH), low),
            pltpu.VMEM((LEN, 2 * CH), low),
            pltpu.VMEM((LEN, CH), low),
            pltpu.VMEM((CH, LEN), low),
            pltpu.VMEM((SIZE, LEN), wide),
            pltpu.VMEM((SIZE, LEN), wide),
            pltpu.VMEM((SIZE, LEN), wide),
            pltpu.VMEM((SIZE, LEN), wide),
            pltpu.VMEM((tokens, CH), wide),
            pltpu.VMEM((NUM_HEADS, CH, CH), wide),
            pltpu.VMEM((CH, CH), wide),
            pltpu.VMEM((PLANE, 17, CH), wide),
            pltpu.VMEM((PLANE, 17, CH), wide),
            pltpu.VMEM((DEPTH, 17, CH), wide),
            pltpu.VMEM((PLANE, 17, CH), wide),
            dma((2,)), dma((2,)), dma((2, 2)), dma((2, 2)),
            dma((PLANE,)), dma((PLANE,)), dma((DEPTH,)), dma((DEPTH,)), dma((PLANE,)), dma((PLANE,)),
        ],
        compiler_params=pltpu.CompilerParams(
            collective_id=0, has_side_effects=True, vmem_limit_bytes=60 << 20
        ),
    )(features.reshape(tokens, CH), grad_out.reshape(tokens, CH), qkv_weight, proj_weight, lepe_weight)
    return grad_features.reshape(features.shape), grad_qkv, grad_proj, grad_lepe


def solution(mesh):
    in_specs = (P("batch", "rows", None, None), P("batch", "rows", None, None), P(), P(), P())
    out_specs = (P("batch", "rows", None, None), P(), P(), P())
    return jax.shard_map(body, mesh=mesh, in_specs=in_specs, out_specs=out_specs, check_vma=False)
```

time: 145 us -> 95.6 us (0.66)
  waiting for transfers between devices: 26.6 us -> 0 us
  starting transfers between devices: 23.2 us -> 0 us
  Pallas kernels: 71.8 us -> 90.7 us
  local copies, waits for them, and re-layouts: 16.2 us -> 4.07 us
  other arithmetic: 5.44 us -> 0 us
    all_to_all x2 -> x0, waiting for transfers between devices: 26.6 us -> none  [the longest x1 26.6 us: body(): lax.all_to_all(sent, 'rows', split_axis=0, concat_axis=0, tiled=True)]
    all_to_all x2 -> x0, starting transfers between devices: 23.2 us -> none  [the longest x1 16.5 us: body(): lax.all_to_all(sent, 'rows', split_axis=0, concat_axis=0, tiled=True)]
    pallas_call x4 -> x1, Pallas kernels: 71.8 us -> 90.7 us  [body(): pl.pallas_call(kernel, in_specs=[vmem] * 5, out_specs=[vmem] * 4, out_sha...]
    reshape x4 -> x0, local copies, waits for them, and re-layouts: 5.92 us -> none  [the longest x1 2.29 us: body(): gt_v.reshape(stripes, owners, band_rows * STRIPE, 3 * half)]
    transpose x5 -> x0, other arithmetic: 2.54 us -> none  [the longest x2 1.25 us: direction(): return (w_nat, w_nat.T, proj_weight[first:first + half], taps)]
    concatenate x3 -> x0, local copies, waits for them, and re-layouts: 2.28 us -> none  [the longest x2 1.48 us: direction(): jnp.concatenate([qkv_weight[:, c + first:c + first + half] for c in (0, c...]
    slice x14 -> x0, local copies, waits for them, and re-layouts: 2.01 us -> none  [the longest x1 0.63 us: body(): flat[6 * half:]]
    concatenate x3 -> x0, other arithmetic: 1.87 us -> none  [the longest x1 1.08 us: body(): sent = jnp.concatenate([pack(features), pack(grad_out)], axis=1)]
  transfers between devices with their start and end apart: 2 -> 0, of which waited for: 1 -> 0; matrix products, arithmetic and copies ran while one was open for 8% -> 0% of each run, Pallas kernels for 34% -> 0%
where the time goes in v2:
time: 95.6 us; the launch traced here: 95.4 us
  Pallas kernels  90.7 us (95%)
  local copies, waits for them, and re-layouts  4.07 us (4%)
    pallas_call x1, Pallas kernels, body(): pl.pallas_call(kernel, in_specs=[vmem] * 5, out_specs=[vmem] * 4, out_sha...  90.7 us
    unnamed x10, local copies, waits for them, and re-layouts  4.07 us

profile of v2, /device:TPU:1, one launch (start us, length us, event | category | flops | bytes accessed | tf_op | source)
XLA Modules:
  0.0 95.4 jit_solution(13545953796836185414)
XLA Ops:
  0.6 90.7 %shard_map.84 = (bf16[2048,128]{1,0:T(8,128)(2,1)}, f32[128,384]{1,0:T(8,128)}, f32[128,128]{1,0:T(8,128)}, f32[9,128]{1,0:T(8,128)}) custom-call(bf16[2048,128]{1,0:T(8,128)(2,1)} %bitcast.3, bf16[2048,128]{1,0:T(8,128)(2,1)} %bitcast.4, bf16[128,384]{1,0:T(8,128)(2,1)} %qkv_ref.1, bf16[128,128]{1,0:T(8,128)(2,1)} %proj_ref.1, bf16[9,128]{1,0:T(8,128)(2,1)} %lepe_ref.1), custom_call_target="tpu_custom_call" | custom-call | tf_op jit(solution)/shard_map/pallas_call | solution.py:393
  91.3 0.0 copy-start
  91.4 1.9 %copy.13 = bf16[1,4,512,128]{3,2,1,0:T(8,128)(2,1)} copy(bf16[1,4,512,128]{3,2,1,0:T(8,128)(2,1)} %bitcast.5) | data formatting | bytes 1048576
  93.3 0.0 copy-done
  93.3 0.0 copy-start.1
  93.3 0.7 copy.14
  94.0 0.2 copy-done.1
  94.1 0.0 copy-start.2
  94.1 0.6 copy.15
  94.8 0.1 copy-done.2
  94.8 0.6 copy.16
Async XLA Ops:
  91.3 1.9 %copy-start = (f32[128,384]{1,0:T(8,128)S(1)}, f32[128,384]{1,0:T(8,128)}, u32[]{:S(2)}) copy-start(f32[128,384]{1,0:T(8,128)} %get-tuple-element.17) | copy-start | bytes 589828
  93.3 0.9 copy-start.1
  94.1 0.7 copy-start.2

commit v3 on v2

--- a/solution.py
+++ b/solution.py
@@ -119,7 +119,7 @@
     x_ref, g_ref, qkv_ref, proj_ref, lepe_ref,
     gf_out, qkv_out, proj_out, lepe_out,
     w_tra, taps, sent, arrived, back, returned, pair, nat, tra, out_s, dq_s, dk_s, dv_s, unit_h, acc, tap_acc,
-    parts, plane_buf, depth_buf, total,
+    parts_h, plane_h, depth_h, total_h, parts_v, plane_v, depth_v, total_v, unit_s, inv_s,
     send_f, recv_f, send_r, recv_r, send_a, recv_a, send_b, recv_b, send_c, recv_c,
 ):
     row = lax.axis_index("rows")
@@ -203,6 +203,81 @@
             send_sem=send_r.at[stripe, head], recv_sem=recv_r.at[stripe, head],
             device_id=((row + 1) % OWNERS, batch), device_id_type=MESH,
         )
+
+    bufs = ((parts_h, plane_h, depth_h, total_h), (parts_v, plane_v, depth_v, total_v))
+
+    def copy_a(side, other, slot):
+        return pltpu.make_async_remote_copy(
+            src_ref=bufs[side][0].at[other], dst_ref=bufs[side][1].at[slot],
+            send_sem=send_a.at[side, other], recv_sem=recv_a.at[side, slot],
+            device_id=plane_peer(other), device_id_type=MESH,
+        )
+
+    def copy_b(side, other, slot):
+        return pltpu.make_async_remote_copy(
+            src_ref=bufs[side][2].at[level], dst_ref=bufs[side][2].at[slot],
+            send_sem=send_b.at[side, other], recv_sem=recv_b.at[side, slot],
+            device_id=depth_peer(other), device_id_type=MESH,
+        )
+
+    def copy_c(side, other, slot):
+        return pltpu.make_async_remote_copy(
+            src_ref=bufs[side][3].at[mine], dst_ref=bufs[side][3].at[slot],
+            send_sem=send_c.at[side, other], recv_sem=recv_c.at[side, slot],
+            device_id=plane_peer(other), device_id_type=MESH,
+        )
+
+    def start_a(side):
+        parts, plane = bufs[side][:2]
+        for index in range(PLANE):
+            head, place = 2 * side + index // 16, index % 16
+            parts[index, :8, :] = acc[head, place * 8 : (place + 1) * 8, :]
+        if side == 1:
+            tap_rows = tap_acc[...].T
+            for index in range(9):
+                parts[index, 8:, :] = tap_rows[index : index + 1, :]
+            for index in range(9, PLANE):
+                parts[index, 8:, :] = jnp.zeros((1, CH), jnp.float32)
+
+        @pl.loop(1, PLANE)
+        def _(step):
+            copy_a(side, (mine + step) % PLANE, mine).start()
+
+        plane[mine] = parts[mine]
+
+    def start_b(side):
+        _, plane, depth, _ = bufs[side]
+
+        @pl.loop(1, PLANE)
+        def _(step):
+            other = (mine + step) % PLANE
+            copy_a(side, other, other).wait_recv()
+
+        sums = [plane[index] for index in range(PLANE)]
+        while len(sums) > 1:
+            sums = [one + two for one, two in zip(sums[::2], sums[1::2])]
+        depth[level] = sums[0]
+
+        @pl.loop(1, DEPTH)
+        def _(step):
+            copy_b(side, (level + step) % DEPTH, level).start()
+
+    def start_c(side):
+        _, _, depth, total = bufs[side]
+
+        @pl.loop(1, DEPTH)
+        def _(step):
+            other = (level + step) % DEPTH
+            copy_b(side, other, other).wait_recv()
+
+        sums = [depth[index] for index in range(DEPTH)]
+        while len(sums) > 1:
+            sums = [one + two for one, two in zip(sums[::2], sums[1::2])]
+        total[mine] = sums[0]
+
+        @pl.loop(1, PLANE)
+        def _(step):
+            copy_c(side, (mine + step) % PLANE, mine).start()
 
     for stripe in range(2):
 
@@ -250,12 +325,22 @@
             else:
                 unit_h[pl.ds(base, LEN), :] += share
 
+    start_a(0)
+
+    @pl.loop(0, 2)
+    def _(turn):
         all_forward(turn).wait_recv()
         unit, _ = normalise(arrived[turn, :, :, :CH].astype(jnp.float32).reshape(LEN, CH))
         pair[:, :CH] = unit.astype(jnp.bfloat16)
         pair[:, CH:] = arrived[turn, :, :, CH:].astype(jnp.float32).reshape(LEN, CH).astype(jnp.bfloat16)
         for head in range(2):
             whole = one_head(2 + head, True)
+            if head == 1:
+
+                @pl.when(turn == 1)
+                def _():
+                    start_a(1)
+
             back[turn, head] = whole.astype(jnp.float32).T.reshape(OWNERS, 8, CH).astype(jnp.bfloat16)
 
             @pl.loop(1, OWNERS)
@@ -264,66 +349,18 @@
 
             returned[turn, head, row] = back[turn, head, row]
 
-    tap_rows = tap_acc[...].T
-    for index in range(PLANE):
-        head, place = index // 8, index % 8
-        parts[index, :16, :] = acc[head, place * 16 : (place + 1) * 16, :]
-        if index < 9:
-            parts[index, 16:, :] = tap_rows[index : index + 1, :]
-        else:
-            parts[index, 16:, :] = jnp.zeros((1, CH), jnp.float32)
-
-    def copy_a(other, slot):
-        return pltpu.make_async_remote_copy(
-            src_ref=parts.at[other], dst_ref=plane_buf.at[slot], send_sem=send_a.at[other], recv_sem=recv_a.at[slot],
-            device_id=plane_peer(other), device_id_type=MESH,
-        )
-
-    def copy_b(other, slot):
-        return pltpu.make_async_remote_copy(
-            src_ref=depth_buf.at[level], dst_ref=depth_buf.at[slot], send_sem=send_b.at[other], recv_sem=recv_b.at[slot],
-            device_id=depth_peer(other), device_id_type=MESH,
-        )
-
-    def copy_c(other, slot):
-        return pltpu.make_async_remote_copy(
-            src_ref=total.at[mine], dst_ref=total.at[slot], send_sem=send_c.at[other], recv_sem=recv_c.at[slot],
-            device_id=plane_peer(other), device_id_type=MESH,
-        )
-
-    @pl.loop(1, PLANE)
-    def _(step):
-        copy_a((mine + step) % PLANE, mine).start()
-
-    plane_buf[mine] = parts[mine]
-
-    @pl.loop(1, PLANE)
-    def _(step):
-        other = (mine + step) % PLANE
-        copy_a(other, other).wait_recv()
-
-    sum_a = plane_buf[0]
-    for index in range(1, PLANE):
-        sum_a = sum_a + plane_buf[index]
-    depth_buf[level] = sum_a
-
-    @pl.loop(1, DEPTH)
-    def _(step):
-        copy_b((level + step) % DEPTH, level).start()
-
-    @pl.loop(1, DEPTH)
-    def _(step):
-        other = (level + step) % DEPTH
-        copy_b(other, other).wait_recv()
-
-    sum_b = depth_buf[0]
-    for index in range(1, DEPTH):
-        sum_b = sum_b + depth_buf[index]
-    total[mine] = sum_b
-
-    @pl.loop(1, PLANE)
-    def _(step):
-        copy_c((mine + step) % PLANE, mine).start()
+        @pl.when(turn == 0)
+        def _():
+            start_b(0)
+
+    start_c(0)
+    for index in range((BAND * WIDTH) // 256):
+        place = slice(index * 256, (index + 1) * 256)
+        unit, inv_std = normalise(x_ref[place, :].astype(jnp.float32))
+        unit_s[place, :] = unit
+        inv_s[place, :] = jnp.broadcast_to(inv_std, (256, CH))
+    start_b(1)
+    start_c(1)
 
     for stripe in range(2):
         for head in range(2):
@@ -346,43 +383,53 @@
         grad_v = dot(ordered, weights)
         for r in range(BAND):
             place = pl.ds(pl.multiple_of(r * WIDTH + q * PIECE, PIECE), PIECE)
-            unit, inv_std = normalise(x_ref[place, :].astype(jnp.float32))
+            unit, inv_std = unit_s[place, :], inv_s[place, :]
             grad_unit = unit_h[place, :] + grad_v[r * PIECE : (r + 1) * PIECE, :]
             mean = jnp.mean(grad_unit, axis=1, keepdims=True)
             along = jnp.mean(grad_unit * unit, axis=1, keepdims=True)
             grad_norm = (grad_unit - mean - unit * along) * inv_std
             gf_out[place, :] = (g_ref[place, :].astype(jnp.float32) + grad_norm).astype(jnp.bfloat16)
 
-    @pl.loop(1, PLANE)
-    def _(step):
-        other = (mine + step) % PLANE
-        copy_c(other, other).wait_recv()
+    for side in range(2):
+
+        @pl.loop(1, PLANE)
+        def _(step):
+            other = (mine + step) % PLANE
+            copy_c(side, other, other).wait_recv()
 
     z = (2 * 512 * 512) ** (-0.5)
 
     def rows_of(head, start):
-        return [total[head * 8 + (start + half * 16) // 16, :16, :] for half in range(2)]
+        total = bufs[head // 2][3]
+        return [total[(head % 2) * 16 + start // 8 + part, :8, :] for part in range(SIZE // 8)]
 
     for part in range(3):
         pieces = [piece for head in range(NUM_HEADS) for piece in rows_of(head, part * SIZE)]
         qkv_out[:, part * CH : (part + 1) * CH] = jnp.concatenate(pieces, axis=0).T * z
     proj_out[...] = jnp.concatenate([piece for head in range(NUM_HEADS) for piece in rows_of(head, 3 * SIZE)], axis=0) * z
-    lepe_out[...] = jnp.concatenate([total[index, 16:, :] for index in range(9)], axis=0) * z
+    lepe_out[...] = jnp.concatenate([total_v[index, 8:, :] for index in range(9)], axis=0) * z
 
     for stripe in range(2):
         all_forward(stripe).wait_send()
         for head in range(2):
             all_backward(stripe, head).wait_send()
 
-    @pl.loop(1, PLANE)
-    def _(step):
-        other = (mine + step) % PLANE
-        copy_a(other, mine).wait_send()
-        copy_c(other, mine).wait_send()
-
-    @pl.loop(1, DEPTH)
-    def _(step):
-        copy_b((level + step) % DEPTH, level).wait_send()
+    for side in range(2):
+
+        @pl.loop(1, PLANE)
+        def _(step):
+            other = (mine + step) % PLANE
+            copy_a(side, other, mine).wait_send()
+            copy_c(side, other, mine).wait_send()
+
+        @pl.loop(1, DEPTH)
+        def _(step):
+            copy_b(side, (level + step) % DEPTH, level).wait_send()
+
+
+def hand_over(*refs):
+    for source, target in zip(refs[:4], refs[4:]):
+        target[...] = source[...]
 
 
 def body(features, grad_out, qkv_weight, proj_weight, lepe_weight):
@@ -417,18 +464,30 @@
             pltpu.VMEM((tokens, CH), wide),
             pltpu.VMEM((NUM_HEADS, CH, CH), wide),
             pltpu.VMEM((CH, CH), wide),
-            pltpu.VMEM((PLANE, 17, CH), wide),
-            pltpu.VMEM((PLANE, 17, CH), wide),
-            pltpu.VMEM((DEPTH, 17, CH), wide),
-            pltpu.VMEM((PLANE, 17, CH), wide),
+            pltpu.VMEM((PLANE, 8, CH), wide),
+            pltpu.VMEM((PLANE, 8, CH), wide),
+            pltpu.VMEM((DEPTH, 8, CH), wide),
+            pltpu.VMEM((PLANE, 8, CH), wide),
+            pltpu.VMEM((PLANE, 9, CH), wide),
+            pltpu.VMEM((PLANE, 9, CH), wide),
+            pltpu.VMEM((DEPTH, 9, CH), wide),
+            pltpu.VMEM((PLANE, 9, CH), wide),
+            pltpu.VMEM((tokens, CH), wide),
+            pltpu.VMEM((tokens, CH), wide),
             dma((2,)), dma((2,)), dma((2, 2)), dma((2, 2)),
-            dma((PLANE,)), dma((PLANE,)), dma((DEPTH,)), dma((DEPTH,)), dma((PLANE,)), dma((PLANE,)),
+            dma((2, PLANE)), dma((2, PLANE)), dma((2, DEPTH)), dma((2, DEPTH)), dma((2, PLANE)), dma((2, PLANE)),
         ],
         compiler_params=pltpu.CompilerParams(
             collective_id=0, has_side_effects=True, vmem_limit_bytes=60 << 20
         ),
     )(features.reshape(tokens, CH), grad_out.reshape(tokens, CH), qkv_weight, proj_weight, lepe_weight)
-    return grad_features.reshape(features.shape), grad_qkv, grad_proj, grad_lepe
+    results = pl.pallas_call(
+        hand_over,
+        in_specs=[vmem] * 4,
+        out_specs=[vmem] * 4,
+        out_shape=[jax.ShapeDtypeStruct(a.shape, a.dtype) for a in (grad_features, grad_qkv, grad_proj, grad_lepe)],
+    )(grad_features, grad_qkv, grad_proj, grad_lepe)
+    return (results[0].reshape(features.shape), *results[1:])
 
 
 def solution(mesh):

time: 95.6 us -> 87.4 us (0.914)
  Pallas kernels: 90.7 us -> 86.6 us
  local copies, waits for them, and re-layouts: 4.07 us -> 0 us
    pallas_call x1, Pallas kernels: 90.7 us -> 84.6 us  [body(): pl.pallas_call(kernel, in_specs=[vmem] * 5, out_specs=[vmem] * 4, out_sha...]
    unnamed x10 -> x0, local copies, waits for them, and re-layouts: 4.07 us -> none
    pallas_call x0 -> x1, Pallas kernels: none -> 2.04 us  [body(): pl.pallas_call(hand_over, in_specs=[vmem] * 4, out_specs=[vmem] * 4, out_...]
where the time goes in v3:
time: 87.4 us; the launch traced here: 87.2 us
  Pallas kernels  86.6 us (99%)
    pallas_call x1, Pallas kernels, body(): pl.pallas_call(kernel, in_specs=[vmem] * 5, out_specs=[vmem] * 4, out_sha...  84.6 us
    pallas_call x1, Pallas kernels, body(): pl.pallas_call(hand_over, in_specs=[vmem] * 4, out_specs=[vmem] * 4, out_...  2.04 us

profile of v3, /device:TPU:1, one launch (start us, length us, event | category | flops | bytes accessed | tf_op | source)
XLA Modules:
  0.0 87.2 jit_solution(15196993587289963596)
XLA Ops:
  0.6 84.6 %shard_map.84 = (bf16[2048,128]{1,0:T(8,128)(2,1)}, f32[128,384]{1,0:T(8,128)}, f32[128,128]{1,0:T(8,128)}, f32[9,128]{1,0:T(8,128)}) custom-call(bf16[2048,128]{1,0:T(8,128)(2,1)} %bitcast.3, bf16[2048,128]{1,0:T(8,128)(2,1)} %bitcast.4, bf16[128,384]{1,0:T(8,128)(2,1)} %qkv_ref.1, bf16[128,128]{1,0:T(8,128)(2,1)} %proj_ref.1, bf16[9,128]{1,0:T(8,128)(2,1)} %lepe_ref.1), custom_call_target="tpu_custom_call" | custom-call | tf_op jit(solution)/shard_map/pallas_call | solution.py:440
  85.2 2.0 %shard_map.85 = (bf16[2048,128]{1,0:T(8,128)(2,1)}, f32[128,384]{1,0:T(8,128)}, f32[128,128]{1,0:T(8,128)}, f32[9,128]{1,0:T(8,128)}) custom-call(bf16[2048,128]{1,0:T(8,128)(2,1)} %get-tuple-element.12.refs_0_, f32[128,384]{1,0:T(8,128)} %get-tuple-element.13.refs_1_, f32[128,128]{1,0:T(8,128)} %get-tuple-element.14.refs_2_, f32[9,128]{1,0:T(8,128)} %get-tuple-element.15.refs_3_), custom_call_target="tpu_custom_call" | custom-call | tf_op jit(solution)/shard_map/pallas_call | solution.py:484

commit v4 on v3

--- a/solution.py
+++ b/solution.py
@@ -12,7 +12,7 @@
 COLS = (((1,), (1,)), ((), ()))
 ROWS = (((0,), (0,)), ((), ()))
 MESH = pl.DeviceIdType.MESH
-QUERY_BLOCK = 512
+QUERY_BLOCK = 1024
 CH = 128
 SIZE = 32
 LEN = 1024
@@ -48,8 +48,8 @@
         probs_low = probs.astype(jnp.bfloat16)
         inner = jnp.sum(probs * d_probs, axis=1, keepdims=True)
         d_scores = (probs * (d_probs - inner) * SCALE).astype(jnp.bfloat16)
-        out_s[:, rows] = dot(v_tra, probs_low, COLS)
-        dq_s[:, rows] = dot(k_tra, d_scores, COLS)
+        out_s[:, rows] = dot(probs_low, nat[:, 2 * SIZE : 3 * SIZE]).T
+        dq_s[:, rows] = dot(d_scores, nat[:, SIZE : 2 * SIZE]).T
         dv_part = dot(tra[3 * SIZE :, rows], probs_low)
         dk_part = dot(tra[:SIZE, rows], d_scores)
         if step == 0:

time: 87.4 us -> 85.3 us (0.976)
  Pallas kernels: 86.6 us -> 84.6 us
    pallas_call x1, Pallas kernels: 84.6 us -> 82.5 us  [body(): pl.pallas_call(kernel, in_specs=[vmem] * 5, out_specs=[vmem] * 4, out_sha...]
where the time goes in v4:
time: 85.3 us; the launch traced here: 85.2 us
  Pallas kernels  84.6 us (99%)
    pallas_call x1, Pallas kernels, body(): pl.pallas_call(kernel, in_specs=[vmem] * 5, out_specs=[vmem] * 4, out_sha...  82.5 us
    pallas_call x1, Pallas kernels, body(): pl.pallas_call(hand_over, in_specs=[vmem] * 4, out_specs=[vmem] * 4, out_...  2.04 us

profile of v4, /device:TPU:1, one launch (start us, length us, event | category | flops | bytes accessed | tf_op | source)
XLA Modules:
  0.0 85.2 jit_solution(4309043321241177364)
XLA Ops:
  0.6 82.5 %shard_map.84 = (bf16[2048,128]{1,0:T(8,128)(2,1)}, f32[128,384]{1,0:T(8,128)}, f32[128,128]{1,0:T(8,128)}, f32[9,128]{1,0:T(8,128)}) custom-call(bf16[2048,128]{1,0:T(8,128)(2,1)} %bitcast.3, bf16[2048,128]{1,0:T(8,128)(2,1)} %bitcast.4, bf16[128,384]{1,0:T(8,128)(2,1)} %qkv_ref.1, bf16[128,128]{1,0:T(8,128)(2,1)} %proj_ref.1, bf16[9,128]{1,0:T(8,128)(2,1)} %lepe_ref.1), custom_call_target="tpu_custom_call" | custom-call | tf_op jit(solution)/shard_map/pallas_call | solution.py:440
  83.2 2.0 %shard_map.85 = (bf16[2048,128]{1,0:T(8,128)(2,1)}, f32[128,384]{1,0:T(8,128)}, f32[128,128]{1,0:T(8,128)}, f32[9,128]{1,0:T(8,128)}) custom-call(bf16[2048,128]{1,0:T(8,128)(2,1)} %get-tuple-element.12.refs_0_, f32[128,384]{1,0:T(8,128)} %get-tuple-element.13.refs_1_, f32[128,128]{1,0:T(8,128)} %get-tuple-element.14.refs_2_, f32[9,128]{1,0:T(8,128)} %get-tuple-element.15.refs_3_), custom_call_target="tpu_custom_call" | custom-call | tf_op jit(solution)/shard_map/pallas_call | solution.py:484
